TPU v7x, 128 devices: a whole 4x4x4 slice. The times are simulated.
128 devices in a mesh: rt: 32 (over x_lo, z, y), mob: 4 (over x_hi, core).
Axes of the slice: x: 4 (x_hi: 2, x_lo: 2; x = x_hi * 2 + x_lo), y: 4, z: 4, core: 2. Of those that a mesh axis runs over, the one named last changes fastest.
Arguments:
- observed: float32 [1024, 64, 1280], P('rt', 'mob'), as said below
- frame_kernel: float32 [31], replicated, may hold values from 0.05 to 1
- scan_kernel: float32 [15], replicated, may hold values from 0.05 to 1
- prec_window: int32 [256], P('rt'), may hold values from 0 to 15
- frag_window: int32 [1024], P('mob'), may hold values from 0 to 15
Outputs:
- estimate: float32 [1024, 64, 1280], P('rt', 'mob')
- correlation: float32 [256, 1024], P('rt', 'mob')
Inputs may be any that keep to these rules, and one draw needn't show every extreme that they name: `observed`: positive intensities.
All inputs are finite; a program needn't handle non-finite values.
Results may differ from a plain program's by a relative error of at most 0.0003.
Values sent between devices are 32-bit elements; how exact they have to be, the bound alone decides.
No kernel may reach another device: no remote copies, remote signals or barrier semaphores. Data moves between devices by JAX's collectives and lax.ppermute only.
A program may use at most 64 MiB of HBM per device.

v0:
```python
import jax
import jax.numpy as jnp
from jax import lax
from jax.sharding import PartitionSpec as P

PREC = 256
ITERS = 2


def extended(cells, sides, width):
    for axis, dim in sides:
        count = lax.axis_size(axis)
        ends = count - 1
        head = lax.slice_in_dim(cells, 0, width, axis=dim)
        tail = lax.slice_in_dim(cells, cells.shape[dim] - width, cells.shape[dim], axis=dim)
        cells = jnp.concatenate(
            [
                lax.ppermute(tail, axis, [(i, (i + 1) % count) for i in range(ends)]),
                cells,
                lax.ppermute(head, axis, [((i + 1) % count, i) for i in range(ends)]),
            ],
            axis=dim,
        )
    return cells


def apply_taps(padded, kernel, along, length):
    running = kernel[0] * lax.slice_in_dim(padded, 0, length, axis=along)
    for tap_index in range(1, kernel.shape[0]):
        running = running + kernel[tap_index] * lax.slice_in_dim(
            padded, tap_index, tap_index + length, axis=along
        )
    return running


def local(observed, frame_kernel, scan_kernel, prec_window, frag_window):
    frames, scan_count, channels = observed.shape
    frame_radius = (frame_kernel.shape[0] - 1) // 2
    scan_radius = (scan_kernel.shape[0] - 1) // 2
    flip_frames = frame_kernel[::-1]
    flip_scans = scan_kernel[::-1]
    estimate = observed
    for iteration in range(ITERS):
        padded_scans = extended(estimate, (("mob", 1),), scan_radius)
        scan_blurred = apply_taps(padded_scans, scan_kernel, 1, scan_count)
        padded_frames = extended(scan_blurred, (("rt", 0),), frame_radius)
        blurred_image = apply_taps(padded_frames, frame_kernel, 0, frames)
        ratio_field = observed / blurred_image
        ratio_frames = extended(ratio_field, (("rt", 0),), frame_radius)
        scan_padded_scans = extended(
            apply_taps(ratio_frames, flip_frames, 0, frames), (("mob", 1),), scan_radius
        )
        estimate = estimate * apply_taps(scan_padded_scans, flip_scans, 1, scan_count)
    profiles = estimate.reshape(frames * scan_count, channels)
    cell_count = frames * scan_count * lax.axis_size("rt") * lax.axis_size("mob")
    channel_total = lax.psum(jnp.sum(profiles, axis=0), ("rt", "mob"))
    channel_mean = channel_total / cell_count
    centered = (profiles - channel_mean).astype(jnp.bfloat16)
    as_float = centered.astype(jnp.float32)
    squares = lax.psum(jnp.sum(as_float * as_float, axis=0), ("rt", "mob"))
    cross_sums = lax.dot_general(
        centered[:, :PREC],
        centered[:, PREC:],
        (((0,), (0,)), ((), ())),
        preferred_element_type=jnp.float32,
    )
    partial_value = lax.psum_scatter(cross_sums, "rt", scatter_dimension=0, tiled=True)
    block_sums = lax.psum_scatter(partial_value, "mob", scatter_dimension=1, tiled=True)
    row_count = prec_window.shape[0]
    column_count = frag_window.shape[0]
    inverse_norm = 1.0 / jnp.sqrt(squares + 1e-06)
    row_inverse = lax.dynamic_slice_in_dim(
        inverse_norm[:PREC], lax.axis_index("rt") * row_count, row_count
    )
    column_inverse = lax.dynamic_slice_in_dim(
        inverse_norm[PREC:], lax.axis_index("mob") * column_count, column_count
    )
    pair_mask = (prec_window[:, None] == frag_window[None, :]).astype(jnp.float32)
    correlation = pair_mask * block_sums * row_inverse[:, None] * column_inverse[None, :]
    return (estimate, correlation)


def solution(mesh):
    placed = (P("rt", "mob", None), P(), P(), P("rt"), P("mob"))
    return jax.shard_map(
        local,
        mesh=mesh,
        in_specs=placed,
        out_specs=(P("rt", "mob", None), P("rt", "mob")),
        check_vma=False,
    )
```

profile of v0, /device:TPU:1, one launch (start us, length us, event | category | flops | bytes accessed | tf_op | source)
XLA Modules:
  0.0 732.5 jit_solution(15922620967570289949)
XLA Ops:
  9.5 6.2 collective-permute-start
  18.9 9.5 %collective-permute-done = f32[32,7,1280]{2,0,1:T(8,128)S(1)} collective-permute-done((f32[32,7,1280]{2,0,1:T(8,128)S(1)}, f32[32,7,1280]{2,0,1:T(8,128)S(1)}, u32[]{:S(2)}, u32[]{:S(2)}) %collective-permute-start) | collective-permute-done | bytes 1146912 | tf_op jit(solution)/shard_map/ppermute | solution.py:18
  29.1 5.6 collective-permute-done.1
  35.4 15.1 %fusion.127 = f32[32,16,1280]{2,1,0:T(8,128)S(1)} fusion(f32[32,16,1280]{2,1,0:T(8,128)S(1)} %copy-done, f32[32,7,1280]{2,1,0:T(8,128)S(1)} %copy.17, f32[32,23,1280]{2,1,0:T(8,128)S(1)} %copy_dynamic-update-slice_fusion, f32[]{:T(128)} %bitcast.16, f32[]{:T(128)} %bitcast.15, f32[]{:T(128)} %bitcast.14, f32[]{:T(128)} %bitcast.13, f32[]{:T(128)} %bitcast.12, ...), kind=kLoop, calls=%fused_computation.435 | loop fusion | flops 23592960 | bytes 24739900 | tf_op jit(solution)/shard_map/add | solution.py:30
  56.7 10.9 %collective-permute-done.2 = f32[15,16,1280]{2,1,0:T(8,128)S(1)} collective-permute-done((f32[15,16,1280]{2,1,0:T(8,128)S(1)}, f32[15,16,1280]{2,1,0:T(8,128)S(1)}, u32[]{:S(2)}, u32[]{:S(2)}) %collective-permute-start.2) | collective-permute-done | bytes 1228832 | tf_op jit(solution)/shard_map/ppermute | solution.py:18
  72.5 34.5 %fusion.405 = f32[32,16,1280]{2,1,0:T(8,128)} fusion(f32[32,16,1280]{2,1,0:T(8,128)S(1)} %copy-done, f32[32,16,1280]{2,1,0:T(8,128)S(1)} %fusion.127, f32[15,16,1280]{2,1,0:T(8,128)} %copy-done.5, f32[15,16,1280]{2,1,0:T(8,128)S(1)} %collective-permute-done.2, f32[]{:T(128)} %bitcast.45, f32[]{:T(128)} %bitcast.44, f32[]{:T(128)} %bitcast.43, f32[]{:T(128)} %bitcast.42, ...), kind=kLoop, calls=%fused_computation.713 | loop fusion | flops 60293120 | bytes 10322044 | tf_op jit(solution)/shard_map/div | solution.py:48
  113.3 13.4 %collective-permute-done.4 = f32[15,16,1280]{2,1,0:T(8,128)S(1)} collective-permute-done((f32[15,16,1280]{2,1,0:T(8,128)S(1)}, f32[15,16,1280]{2,1,0:T(8,128)S(1)}, u32[]{:S(2)}, u32[]{:S(2)}) %collective-permute-start.4) | collective-permute-done | bytes 1228832 | tf_op jit(solution)/shard_map/ppermute | solution.py:18
  130.9 53.8 %fusion.318 = f32[32,16,1280]{2,1,0:T(8,128)S(1)} fusion(f32[32,16,1280]{2,1,0:T(8,128)} %fusion.405, f32[15,16,1280]{2,1,0:T(8,128)} %collective-permute-done.5, f32[15,16,1280]{2,1,0:T(8,128)S(1)} %collective-permute-done.4, f32[]{:T(128)} %bitcast.45, f32[]{:T(128)} %bitcast.44, f32[]{:T(128)} %bitcast.43, f32[]{:T(128)} %bitcast.42, f32[]{:T(128)} %bitcast.41, ...), kind=kLoop, calls=%fused_computation.626 | loop fusion | flops 59637760 | bytes 7700604 | tf_op jit(solution)/shard_map/add | solution.py:30
  192.6 10.0 %collective-permute-done.6 = f32[32,7,1280]{2,0,1:T(8,128)S(1)} collective-permute-done((f32[32,7,1280]{2,0,1:T(8,128)S(1)}, f32[32,7,1280]{2,0,1:T(8,128)S(1)}, u32[]{:S(2)}, u32[]{:S(2)}) %collective-permute-start.6) | collective-permute-done | bytes 1146912 | tf_op jit(solution)/shard_map/ppermute | solution.py:18
  203.3 6.1 collective-permute-done.7
  210.0 16.5 %fusion.81 = f32[32,16,1280]{2,1,0:T(8,128)S(1)} fusion(f32[32,16,1280]{2,1,0:T(8,128)S(1)} %copy-done, f32[32,16,1280]{2,1,0:T(8,128)S(1)} %copy-done.3, f32[32,7,1280]{2,1,0:T(8,128)S(1)} %copy.23, f32[32,7,1280]{2,1,0:T(8,128)S(1)} %copy.21, f32[]{:T(128)} %bitcast.16, f32[]{:T(128)} %bitcast.15, f32[]{:T(128)} %bitcast.14, f32[]{:T(128)} %bitcast.13, ...), kind=kLoop, calls=%fused_computation.389 | loop fusion | flops 28835840 | bytes 10158140 | tf_op jit(solution)/shard_map/mul | solution.py:53
  231.9 9.9 %collective-permute-done.8 = f32[32,7,1280]{2,0,1:T(8,128)S(1)} collective-permute-done((f32[32,7,1280]{2,0,1:T(8,128)S(1)}, f32[32,7,1280]{2,0,1:T(8,128)S(1)}, u32[]{:S(2)}, u32[]{:S(2)}) %collective-permute-start.8) | collective-permute-done | bytes 1146912 | tf_op jit(solution)/shard_map/ppermute | solution.py:18
  242.5 5.6 collective-permute-done.9
  248.8 16.3 %fusion.42 = f32[32,16,1280]{2,1,0:T(8,128)S(1)} fusion(f32[32,16,1280]{2,1,0:T(8,128)S(1)} %fusion.81, f32[32,7,1280]{2,1,0:T(8,128)S(1)} %copy.27, f32[32,7,1280]{2,1,0:T(8,128)S(1)} %copy.25, f32[]{:T(128)} %bitcast.16, f32[]{:T(128)} %bitcast.15, f32[]{:T(128)} %bitcast.14, f32[]{:T(128)} %bitcast.13, f32[]{:T(128)} %bitcast.12, f32[]{:T(128)} %bitcast.11, ...), kind=kLoop, calls=%fused_computation.350 | loop fusion | flops 28180480 | bytes 7536700 | tf_op jit(solution)/shard_map/add | solution.py:30
  272.7 12.5 %collective-permute-done.10 = f32[15,16,1280]{2,1,0:T(8,128)S(1)} collective-permute-done((f32[15,16,1280]{2,1,0:T(8,128)S(1)}, f32[15,16,1280]{2,1,0:T(8,128)S(1)}, u32[]{:S(2)}, u32[]{:S(2)}) %collective-permute-start.10) | collective-permute-done | bytes 1228832 | tf_op jit(solution)/shard_map/ppermute | solution.py:18
  289.4 54.3 %fusion.232 = f32[32,16,1280]{2,1,0:T(8,128)} fusion(f32[32,16,1280]{2,1,0:T(8,128)S(1)} %copy-done, f32[32,16,1280]{2,1,0:T(8,128)} %copy-done.4, f32[15,16,1280]{2,1,0:T(8,128)} %collective-permute-done.11, f32[15,16,1280]{2,1,0:T(8,128)S(1)} %collective-permute-done.10, f32[]{:T(128)} %bitcast.45, f32[]{:T(128)} %bitcast.44, f32[]{:T(128)} %bitcast.43, ...), kind=kLoop, calls=%fused_computation.540 | loop fusion | flops 60293120 | bytes 10322044 | tf_op jit(solution)/shard_map/div | solution.py:48
  350.8 13.4 %collective-permute-done.12 = f32[15,16,1280]{2,1,0:T(8,128)S(1)} collective-permute-done((f32[15,16,1280]{2,1,0:T(8,128)S(1)}, f32[15,16,1280]{2,1,0:T(8,128)S(1)}, u32[]{:S(2)}, u32[]{:S(2)}) %collective-permute-start.12) | collective-permute-done | bytes 1228832 | tf_op jit(solution)/shard_map/ppermute | solution.py:18
  368.8 52.5 %fusion.145 = f32[32,16,1280]{2,1,0:T(8,128)S(1)} fusion(f32[32,16,1280]{2,1,0:T(8,128)} %fusion.232, f32[15,16,1280]{2,1,0:T(8,128)} %collective-permute-done.13, f32[15,16,1280]{2,1,0:T(8,128)S(1)} %collective-permute-done.12, f32[]{:T(128)} %bitcast.45, f32[]{:T(128)} %bitcast.44, f32[]{:T(128)} %bitcast.43, f32[]{:T(128)} %bitcast.42, f32[]{:T(128)} %bitcast.41, ...), kind=kLoop, calls=%fused_computation.453 | loop fusion | flops 59637760 | bytes 7700604 | tf_op jit(solution)/shard_map/add | solution.py:30
  426.7 10.3 %collective-permute-done.14 = f32[32,7,1280]{2,0,1:T(8,128)S(1)} collective-permute-done((f32[32,7,1280]{2,0,1:T(8,128)S(1)}, f32[32,7,1280]{2,0,1:T(8,128)S(1)}, u32[]{:S(2)}, u32[]{:S(2)}) %collective-permute-start.14) | collective-permute-done | bytes 1146912 | tf_op jit(solution)/shard_map/ppermute | solution.py:18
  443.9 17.4 %fusion.507 = (f32[1280]{0:T(1024)S(1)}, f32[32,16,1280]{2,1,0:T(8,128)}) fusion(f32[32,16,1280]{2,1,0:T(8,128)S(1)} %fusion.81, f32[32,7,1280]{2,1,0:T(8,128)S(1)} %copy.31, f32[32,16,1280]{2,1,0:T(8,128)S(1)} %fusion.145, f32[]{:T(128)} %bitcast.3, f32[]{:T(128)} %bitcast.4, f32[]{:T(128)} %bitcast.5, f32[]{:T(128)} %bitcast.6, f32[]{:T(128)} %bitcast.7, ...), kind=kLoop, calls=%fused_computation.845 | loop fusion | flops 29489920 | bytes 10163260 | tf_op jit(solution)/shard_map/reduce_sum | solution.py:56
  461.3 74.5 %psum.14 = f32[1280]{0:T(1024)S(1)} all-reduce(f32[1280]{0:T(1024)S(1)} %get-tuple-element.4), channel_id=1, replica_groups=mesh['rt'=32,'mob'=4] {'rt','mob'}, use_global_device_ids=true, to_apply=%region_1.0 | all-reduce | flops 1280 | bytes 10240 | tf_op jit(solution)/shard_map/psum | solution.py:56
  540.2 64.9 %psum.15 = f32[1280]{0:T(1024)S(1)} all-reduce(f32[1280]{0:T(1024)S(1)} %multiply_reduce_fusion), channel_id=1, replica_groups=mesh['rt'=32,'mob'=4] {'rt','mob'}, use_global_device_ids=true, to_apply=%region_5.0 | all-reduce | flops 1280 | bytes 10240 | tf_op jit(solution)/shard_map/psum | solution.py:60
  605.2 69.0 %reduce-scatter.3.cloned.1.call-done = f32[8,1024]{1,0:T(8,128)} async-done(((f32[256,1024]{1,0:T(8,128)}), f32[8,1024]{1,0:T(8,128)}) %reduce-scatter.3.cloned.1.call-update) | async-done | bytes 32784 | tf_op jit(solution)/shard_map/reduce_scatter | solution.py:67
  674.4 49.9 %reduce-scatter.5.cloned.1.call-done = f32[8,256]{1,0:T(8,128)} async-done(((f32[8,1024]{1,0:T(8,128)}), f32[8,256]{1,0:T(8,128)}) %reduce-scatter.5.cloned.1.call-update) | async-done | bytes 8208 | tf_op jit(solution)/shard_map/reduce_scatter | solution.py:68
  (82 shorter events, 86.0 us)
Async XLA Ops:
  7.2 667.0 %reduce-scatter.3.cloned.1.call-start = ((), (), s32[]{:S(2)}) async-start(), calls=%async_computation.2 | async-start | bytes 1081344 | tf_op jit(solution)/shard_map/reduce_scatter | solution.py:67
  9.1 8.9 %copy-start.7 = (f32[15]{0:T(128)S(1)}, f32[15]{0:T(128)}, u32[]{:S(2)}) copy-start(f32[15]{0:T(128)} %param.7) | copy-start | bytes 184
  9.1 9.6 %copy-start = (f32[32,16,1280]{2,1,0:T(8,128)S(1)}, f32[32,16,1280]{2,1,0:T(8,128)}, u32[]{:S(2)}) copy-start(f32[32,16,1280]{2,1,0:T(8,128)} %param.5) | copy-start | bytes 7864324
  9.5 18.9 %collective-permute-start = (f32[32,7,1280]{2,0,1:T(8,128)S(1)}, f32[32,7,1280]{2,0,1:T(8,128)S(1)}, u32[]{:S(2)}, u32[]{:S(2)}) collective-permute-start(f32[32,7,1280]{2,0,1:T(8,128)S(1)} %copy.32), channel_id=1, source_target_pairs={{0,1},{1,2},{2,3},{4,5},{5,6},{6,7},{8,9},{9,10},{10,11},{12,13},{... | collective-permute-start | bytes 3440648 | tf_op jit(solution)/shard_map/ppermute | solution.py:18
  16.0 18.7 %collective-permute-start.1 = (f32[32,7,1280]{2,0,1:T(8,128)S(1)}, f32[32,7,1280]{2,0,1:T(8,128)S(1)}, u32[]{:S(2)}, u32[]{:S(2)}) collective-permute-start(f32[32,7,1280]{2,0,1:T(8,128)S(1)} %copy.33), channel_id=1, source_target_pairs={{1,0},{2,1},{3,2},{5,4},{6,5},{7,6},{9,8},{10,9},{11,10},{13,12},{... | collective-permute-start | bytes 3440648 | tf_op jit(solution)/shard_map/ppermute | solution.py:20
  50.5 4.8 copy-start.6
  50.7 16.9 %collective-permute-start.2 = (f32[15,16,1280]{2,1,0:T(8,128)S(1)}, f32[15,16,1280]{2,1,0:T(8,128)S(1)}, u32[]{:S(2)}, u32[]{:S(2)}) collective-permute-start(f32[15,16,1280]{2,1,0:T(8,128)S(1)} %get-tuple-element.18), channel_id=1, source_target_pairs={{0,4},{4,8},{8,12},{12,16},{16,20},{20,24},{24,28},{28,32},{32,36}... | collective-permute-start | bytes 3686408 | tf_op jit(solution)/shard_map/ppermute | solution.py:18
  53.9 17.5 %collective-permute-start.3 = (f32[15,16,1280]{2,1,0:T(8,128)S(1)}, f32[15,16,1280]{2,1,0:T(8,128)S(1)}, u32[]{:S(2)}, u32[]{:S(2)}) collective-permute-start(f32[15,16,1280]{2,1,0:T(8,128)S(1)} %get-tuple-element.19), channel_id=1, source_target_pairs={{4,0},{8,4},{12,8},{16,12},{20,16},{24,20},{28,24},{32,28},{36,32}... | collective-permute-start | bytes 3686408 | tf_op jit(solution)/shard_map/ppermute | solution.py:20
  108.8 17.9 %collective-permute-start.4 = (f32[15,16,1280]{2,1,0:T(8,128)S(1)}, f32[15,16,1280]{2,1,0:T(8,128)S(1)}, u32[]{:S(2)}, u32[]{:S(2)}) collective-permute-start(f32[15,16,1280]{2,1,0:T(8,128)S(1)} %get-tuple-element.16), channel_id=1, source_target_pairs={{0,4},{4,8},{8,12},{12,16},{16,20},{20,24},{24,28},{28,32},{32,36}... | collective-permute-start | bytes 3686408 | tf_op jit(solution)/shard_map/ppermute | solution.py:18
  112.0 18.9 %collective-permute-start.5 = (f32[15,16,1280]{2,1,0:T(8,128)S(1)}, f32[15,16,1280]{2,1,0:T(8,128)}, u32[]{:S(2)}, u32[]{:S(2)}) collective-permute-start(f32[15,16,1280]{2,1,0:T(8,128)S(1)} %get-tuple-element.17), channel_id=1, source_target_pairs={{4,0},{8,4},{12,8},{16,12},{20,16},{24,20},{28,24},{32,28},{36,32}... | collective-permute-start | bytes 3686408 | tf_op jit(solution)/shard_map/ppermute | solution.py:20
  186.6 16.0 %collective-permute-start.6 = (f32[32,7,1280]{2,0,1:T(8,128)S(1)}, f32[32,7,1280]{2,0,1:T(8,128)S(1)}, u32[]{:S(2)}, u32[]{:S(2)}) collective-permute-start(f32[32,7,1280]{2,0,1:T(8,128)S(1)} %copy.20), channel_id=1, source_target_pairs={{0,1},{1,2},{2,3},{4,5},{5,6},{6,7},{8,9},{9,10},{10,11},{12,13},{... | collective-permute-start | bytes 3440648 | tf_op jit(solution)/shard_map/ppermute | solution.py:18
  190.4 19.6 %copy-start.3 = (f32[32,16,1280]{2,1,0:T(8,128)S(1)}, f32[32,16,1280]{2,1,0:T(8,128)}, u32[]{:S(2)}) copy-start(f32[32,16,1280]{2,1,0:T(8,128)} %copy-done.2) | copy-start | bytes 7864324
  190.4 18.9 %collective-permute-start.7 = (f32[32,7,1280]{2,0,1:T(8,128)S(1)}, f32[32,7,1280]{2,0,1:T(8,128)S(1)}, u32[]{:S(2)}, u32[]{:S(2)}) collective-permute-start(f32[32,7,1280]{2,0,1:T(8,128)S(1)} %copy.22), channel_id=1, source_target_pairs={{1,0},{2,1},{3,2},{5,4},{6,5},{7,6},{9,8},{10,9},{11,10},{13,12},{... | collective-permute-start | bytes 3440648 | tf_op jit(solution)/shard_map/ppermute | solution.py:20
  227.2 14.7 %collective-permute-start.8 = (f32[32,7,1280]{2,0,1:T(8,128)S(1)}, f32[32,7,1280]{2,0,1:T(8,128)S(1)}, u32[]{:S(2)}, u32[]{:S(2)}) collective-permute-start(f32[32,7,1280]{2,0,1:T(8,128)S(1)} %copy.24), channel_id=1, source_target_pairs={{0,1},{1,2},{2,3},{4,5},{5,6},{6,7},{8,9},{9,10},{10,11},{12,13},{... | collective-permute-start | bytes 3440648 | tf_op jit(solution)/shard_map/ppermute | solution.py:18
  229.5 18.7 %collective-permute-start.9 = (f32[32,7,1280]{2,0,1:T(8,128)S(1)}, f32[32,7,1280]{2,0,1:T(8,128)S(1)}, u32[]{:S(2)}, u32[]{:S(2)}) collective-permute-start(f32[32,7,1280]{2,0,1:T(8,128)S(1)} %copy.26), channel_id=1, source_target_pairs={{1,0},{2,1},{3,2},{5,4},{6,5},{7,6},{9,8},{10,9},{11,10},{13,12},{... | collective-permute-start | bytes 3440648 | tf_op jit(solution)/shard_map/ppermute | solution.py:20
  266.8 18.4 %collective-permute-start.10 = (f32[15,16,1280]{2,1,0:T(8,128)S(1)}, f32[15,16,1280]{2,1,0:T(8,128)S(1)}, u32[]{:S(2)}, u32[]{:S(2)}) collective-permute-start(f32[15,16,1280]{2,1,0:T(8,128)S(1)} %get-tuple-element.10), channel_id=1, source_target_pairs={{0,4},{4,8},{8,12},{12,16},{16,20},{20,24},{24,28},{28,32},{32,36}... | collective-permute-start | bytes 3686408 | tf_op jit(solution)/shard_map/ppermute | solution.py:18
  271.4 18.1 %collective-permute-start.11 = (f32[15,16,1280]{2,1,0:T(8,128)S(1)}, f32[15,16,1280]{2,1,0:T(8,128)}, u32[]{:S(2)}, u32[]{:S(2)}) collective-permute-start(f32[15,16,1280]{2,1,0:T(8,128)S(1)} %get-tuple-element.11), channel_id=1, source_target_pairs={{4,0},{8,4},{12,8},{16,12},{20,16},{24,20},{28,24},{32,28},{36,32}... | collective-permute-start | bytes 3686408 | tf_op jit(solution)/shard_map/ppermute | solution.py:20
  345.6 18.7 %collective-permute-start.12 = (f32[15,16,1280]{2,1,0:T(8,128)S(1)}, f32[15,16,1280]{2,1,0:T(8,128)S(1)}, u32[]{:S(2)}, u32[]{:S(2)}) collective-permute-start(f32[15,16,1280]{2,1,0:T(8,128)S(1)} %get-tuple-element.8), channel_id=1, source_target_pairs={{0,4},{4,8},{8,12},{12,16},{16,20},{20,24},{24,28},{28,32},{32,36}... | collective-permute-start | bytes 3686408 | tf_op jit(solution)/shard_map/ppermute | solution.py:18
  349.3 19.4 %collective-permute-start.13 = (f32[15,16,1280]{2,1,0:T(8,128)S(1)}, f32[15,16,1280]{2,1,0:T(8,128)}, u32[]{:S(2)}, u32[]{:S(2)}) collective-permute-start(f32[15,16,1280]{2,1,0:T(8,128)S(1)} %get-tuple-element.9), channel_id=1, source_target_pairs={{4,0},{8,4},{12,8},{16,12},{20,16},{24,20},{28,24},{32,28},{36,32}... | collective-permute-start | bytes 3686408 | tf_op jit(solution)/shard_map/ppermute | solution.py:20
  421.9 15.1 %collective-permute-start.14 = (f32[32,7,1280]{2,0,1:T(8,128)S(1)}, f32[32,7,1280]{2,0,1:T(8,128)S(1)}, u32[]{:S(2)}, u32[]{:S(2)}) collective-permute-start(f32[32,7,1280]{2,0,1:T(8,128)S(1)} %copy.28), channel_id=1, source_target_pairs={{0,1},{1,2},{2,3},{4,5},{5,6},{6,7},{8,9},{9,10},{10,11},{12,13},{... | collective-permute-start | bytes 3440648 | tf_op jit(solution)/shard_map/ppermute | solution.py:18
  424.6 18.7 %collective-permute-start.15 = (f32[32,7,1280]{2,0,1:T(8,128)S(1)}, f32[32,7,1280]{2,0,1:T(8,128)S(1)}, u32[]{:S(2)}, u32[]{:S(2)}) collective-permute-start(f32[32,7,1280]{2,0,1:T(8,128)S(1)} %copy.30), channel_id=1, source_target_pairs={{1,0},{2,1},{3,2},{5,4},{6,5},{7,6},{9,8},{10,9},{11,10},{13,12},{... | collective-permute-start | bytes 3440648 | tf_op jit(solution)/shard_map/ppermute | solution.py:20
  537.8 186.5 %copy-start.8 = (s32[256]{0:T(256)S(1)}, s32[256]{0:T(256)}, u32[]{:S(2)}) copy-start(s32[256]{0:T(256)} %param.9) | copy-start | bytes 3076
  537.8 186.5 %copy-start.9 = (s32[8]{0:T(128)S(1)}, s32[8]{0:T(128)}, u32[]{:S(2)}) copy-start(s32[8]{0:T(128)} %param.8) | copy-start | bytes 100
  539.3 185.0 %reduce-scatter.5.cloned.1.call-start = ((), (), s32[]{:S(2)}) async-start(), calls=%async_computation.3 | async-start | bytes 40960 | tf_op jit(solution)/shard_map/reduce_scatter | solution.py:68
  (4 other events, 6.2 us)
Sparse Core Ops, SparseCore 0:
  539.4 134.6 reduce-scatter.2
  676.6 47.5 reduce-scatter.4
where the time goes:
time: 735 us; the launch traced here: 733 us
  other arithmetic  264 us (36%)
  waiting for transfers between devices  249 us (34%)
  blocking collectives  139 us (19%)
  starting transfers between devices  42.8 us (6%)
  local copies, waits for them, and re-layouts  21.7 us (3%)
  between operations  14.5 us (2%)
    add x4, other arithmetic, apply_taps(): running + kernel[tap_index] * lax.slice_in_dim(padded, tap_index, tap_ind...  138 us
    ppermute x8, waiting for transfers between devices, extended(): lax.ppermute(tail, axis, [(i, (i + 1) % count) for i in range(ends)])  89.9 us
    div x2, other arithmetic, local(): ratio_field = observed / blurred_image  88.8 us
    psum x1, blocking collectives, local(): channel_total = lax.psum(jnp.sum(profiles, axis=0), ('rt', 'mob'))  74.5 us
    reduce_scatter x1, waiting for transfers between devices, local(): lax.psum_scatter(cross_sums, 'rt', scatter_dimension=0, tiled=True)  69 us
    psum x1, blocking collectives, local(): squares = lax.psum(jnp.sum(as_float * as_float, axis=0), ('rt', 'mob'))  64.9 us
    reduce_scatter x1, waiting for transfers between devices, local(): lax.psum_scatter(partial_value, 'mob', scatter_dimension=1, tiled=True)  49.9 us
    ppermute x8, waiting for transfers between devices, extended(): lax.ppermute(head, axis, [((i + 1) % count, i) for i in range(ends)])  39.8 us
  transfers between devices with their start and end apart: 18, of which 18 were waited for; matrix products, arithmetic and copies ran while one was open for 1% of the time, Pallas kernels for 0%

commit v1 on v0

v1 whole, which is shorter than its diff:
```python
import functools

import jax
import jax.numpy as jnp
from jax import lax
from jax.experimental import pallas as pl
from jax.experimental.pallas import tpu as pltpu
from jax.sharding import PartitionSpec as P

PREC = 256
ITERS = 2
LANES = 128
AXES = ("rt", "mob")
BLOCK = 256
HALO = 128

F32 = jnp.float32
BF16 = jnp.bfloat16


def split(values):
    high = values.astype(BF16)
    return high, (values - high.astype(F32)).astype(BF16)


def taps_at(offset, taps_ref, count):
    out = jnp.zeros(offset.shape, F32)
    for tap in range(count):
        out = jnp.where(offset == tap, taps_ref[tap], out)
    return out


def frame_rows(scan, k, frames, scans, tiles):
    return pl.ds((scan // 8 * tiles + k) * 8 + scan % 8, frames, stride=scans * tiles)


def to_tiles(field):
    frames, scans, channels = field.shape
    field = field.reshape(frames, scans // 8, 8, channels // LANES, LANES).transpose(0, 1, 3, 2, 4)
    return field.reshape(frames * scans * channels // LANES, LANES)


def from_tiles(rows, frames, scans):
    tiles = rows.shape[0] // (frames * scans)
    field = rows.reshape(frames, scans // 8, tiles, 8, LANES).transpose(0, 1, 3, 2, 4)
    return field.reshape(frames, scans, tiles * LANES)


def pack_kernel(
    frame_ref, scan_ref, x_ref, p_ref, wf_ref, wa_ref, sf_ref, sa_ref, *, frames, scans, radii, group
):
    per_lane = LANES // frames
    quads = scans // per_lane
    owners = LANES
    rows = p_ref.shape[0] // owners
    tiles = x_ref.shape[0] // (frames * scans)

    def body(k, carry):
        for q in range(quads):
            block = jnp.concatenate(
                [x_ref[frame_rows(q * per_lane + j, k, frames, scans, tiles), :] for j in range(per_lane)], axis=0
            )
            p_ref[pl.ds(k * quads + q, owners, stride=rows), :] = block.T
        return carry

    lax.fori_loop(0, tiles, body, 0)

    frame_radius, scan_radius = radii
    source = lax.broadcasted_iota(jnp.int32, (BLOCK, BLOCK), 0)
    target = lax.broadcasted_iota(jnp.int32, (BLOCK, BLOCK), 1)
    edge = lax.broadcasted_iota(jnp.int32, (HALO, BLOCK), 0)
    edge = jnp.where(edge < HALO // 2, edge + BLOCK, edge - HALO)
    edge_target = lax.broadcasted_iota(jnp.int32, (HALO, BLOCK), 1)
    for ref, sign in ((wf_ref, 1), (wa_ref, -1)):
        high, low = split(taps_at(sign * (source - target) + frame_radius, frame_ref, 2 * frame_radius + 1))
        edge_high, edge_low = split(
            taps_at(sign * (edge - edge_target) + frame_radius, frame_ref, 2 * frame_radius + 1)
        )
        pieces = (high, high, low, edge_high, edge_high, edge_low)
        at = 0
        for piece in pieces:
            ref[at : at + piece.shape[0], :] = piece
            at += piece.shape[0]
    row = lax.broadcasted_iota(jnp.int32, (group, group), 0)
    col = lax.broadcasted_iota(jnp.int32, (group, group), 1)

    def place(index):
        tile, inner = index // 8, index % 8
        scan = (tile // per_lane) * scans + (inner % quads) * per_lane + tile % per_lane
        return scan, inner // quads

    row_scan, row_channel = place(row)
    col_scan, col_channel = place(col)
    for ref, sign in ((sf_ref, 1), (sa_ref, -1)):
        matrix = jnp.where(
            row_channel == col_channel,
            taps_at(sign * (col_scan - row_scan) + scan_radius, scan_ref, 2 * scan_radius + 1),
            0.0,
        )
        high, low = split(matrix)
        ref[:, 0:group] = high
        ref[:, group : 2 * group] = high
        ref[:, 2 * group : 3 * group] = low


def swap_blocks(tiles, lane, width):
    first, second, third, fourth = tiles
    wide = lane < 2 * width
    narrow = (lane % (2 * width)) < width
    pairs = []
    for a, b in ((first, third), (second, fourth)):
        pairs.append(
            (
                jnp.where(wide, a, pltpu.roll(b, 2 * width, 1)),
                jnp.where(wide, pltpu.roll(a, 2 * width, 1), b),
            )
        )
    out = []
    for a, b in zip(pairs[0], pairs[1]):
        out.append(jnp.where(narrow, a, pltpu.roll(b, width, 1)))
        out.append(jnp.where(narrow, pltpu.roll(a, LANES - width, 1), b))
    return out


def deblur_kernel(p_ref, wf_ref, wa_ref, sf_ref, sa_ref, out_ref, obs_ref, est_ref, mean_ref, *, frames, mobs, rows, cells):
    owners = LANES
    out_rows = out_ref.shape[0] // owners
    blocks, group, width = obs_ref.shape
    per_lane = LANES // frames
    lane = lax.broadcasted_iota(jnp.int32, (8, LANES), 1)
    row8 = lax.broadcasted_iota(jnp.int32, (8, 1), 0)
    halo_lane = lax.broadcasted_iota(jnp.int32, (group, HALO), 1)
    halves = width // LANES
    mean_ref[...] = jnp.zeros_like(mean_ref)

    def scan_blur(values, matrix):
        high, low = split(values)
        return jnp.dot(matrix, jnp.concatenate([high, low, high], axis=0), preferred_element_type=F32)

    def frame_blur(values, matrix):
        parts = [split(v) for v in values]
        lhs = []
        for n in range(blocks):
            center_high, center_low = parts[n]
            halo = []
            for which in (0, 1):
                after = parts[n + 1][which][:, :HALO] if n + 1 < blocks else None
                before = parts[n - 1][which][:, width - HALO :] if n else None
                zero = jnp.zeros((group, HALO), BF16)
                halo.append(
                    jnp.where(
                        halo_lane < HALO // 2,
                        zero if after is None else after,
                        zero if before is None else before,
                    )
                )
            lhs.append(
                jnp.concatenate([center_high, center_low, center_high, halo[0], halo[1], halo[0]], axis=1)
            )
        out = jnp.dot(jnp.concatenate(lhs, axis=0), matrix, preferred_element_type=F32)
        return [out[n * group : (n + 1) * group] for n in range(blocks)]

    def total8(parts):
        acc = None
        for part in parts:
            for half in range(halves):
                piece = part[:, half * LANES : (half + 1) * LANES].reshape(group // 8, 8, LANES).sum(axis=0)
                acc = piece if acc is None else acc + piece
        rows_sum = jnp.sum(acc, axis=1, keepdims=True)
        zero = jnp.zeros_like(rows_sum)
        upper = jnp.sum(jnp.where(row8 < 4, rows_sum, zero), axis=0, keepdims=True)
        lower = jnp.sum(jnp.where(row8 < 4, zero, rows_sum), axis=0, keepdims=True)
        return upper, lower

    def body(pair, carry):
        def at(run, y, mob, stride):
            start = ((run * per_lane + y) * mobs + mob) * stride + pair * 8
            return pl.ds(pl.multiple_of(start, 8), 8)

        for run in range(blocks * halves):
            n, half = run // halves, run % halves
            for mob in range(mobs):
                tiles = [p_ref[at(run, y, mob, rows), :] for y in range(per_lane)]
                for j, tile in enumerate(swap_blocks(tiles, lane, frames)):
                    b = mob * per_lane + j
                    obs_ref[n, b * 8 : b * 8 + 8, half * LANES : (half + 1) * LANES] = tile
                    est_ref[n, b * 8 : b * 8 + 8, half * LANES : (half + 1) * LANES] = tile

        for _ in range(ITERS):
            blurred = frame_blur([scan_blur(est_ref[n], sf_ref[...]) for n in range(blocks)], wf_ref[...])
            ratio = [obs_ref[n] / blurred[n] for n in range(blocks)]
            back = frame_blur(ratio, wa_ref[...])
            for n in range(blocks):
                est_ref[n] = est_ref[n] * scan_blur(back[n], sa_ref[...])

        upper, lower = total8([est_ref[n] for n in range(blocks)])
        upper_mean, lower_mean = upper / cells, lower / cells
        mean8 = jnp.where(row8 < 4, upper_mean, lower_mean)
        squares = []
        for n in range(blocks):
            centered = est_ref[n].reshape(group // 8, 8, width) - mean8[None]
            centered = centered.astype(BF16).astype(F32).reshape(group, width)
            squares.append(centered * centered)
        upper_sq, lower_sq = total8(squares)
        upper_inv = 1.0 / jnp.sqrt(upper_sq + 1e-06)
        lower_inv = 1.0 / jnp.sqrt(lower_sq + 1e-06)
        held = mean_ref[...]
        held = jnp.where(lane == 2 * pair, upper_mean, held)
        held = jnp.where(lane == 2 * pair + 1, lower_mean, held)
        held = jnp.where(lane == LANES // 2 + 2 * pair, upper_inv, held)
        held = jnp.where(lane == LANES // 2 + 2 * pair + 1, lower_inv, held)
        mean_ref[...] = held

        for run in range(blocks * halves):
            n, half = run // halves, run % halves
            for mob in range(mobs):
                tiles = []
                for j in range(per_lane):
                    b = mob * per_lane + j
                    tiles.append(est_ref[n, b * 8 : b * 8 + 8, half * LANES : (half + 1) * LANES])
                for y, tile in enumerate(swap_blocks(tiles, lane, frames)):
                    out_ref[at(run, y, mob, out_rows), :] = tile
        return carry

    lax.fori_loop(0, rows // 8, body, 0)
    for owner in range(owners):
        out_ref[owner * out_rows + rows : owner * out_rows + rows + 8, :] = mean_ref[...]


def unpack_kernel(q_ref, est_ref, cross_ref, centered_ref, *, frames, scans, rows, shards):
    owners = LANES
    stride = q_ref.shape[0] // owners
    per_lane = LANES // frames
    quads = scans // per_lane
    channels = centered_ref.shape[1]
    tiles = channels // LANES
    stats = q_ref[pl.ds(rows, owners, stride=stride), :]
    stats_t = stats.T
    for k in range(channels // LANES):
        lanes = slice(k * LANES, (k + 1) * LANES)
        for q in range(quads):
            block = q_ref[pl.ds(k * quads + q, owners, stride=stride), :].T
            for j in range(per_lane):
                est_ref[frame_rows(q * per_lane + j, k, frames, scans, tiles), :] = block[j * frames : (j + 1) * frames]
            centered_ref[q * LANES : (q + 1) * LANES, lanes] = (block - stats_t[k : k + 1]).astype(BF16)
    row_shards, column_shards = shards
    wide = (channels - PREC) // column_shards
    for m in range(column_shards):
        cross = lax.dot_general(
            centered_ref[:, :PREC],
            centered_ref[:, PREC + m * wide : PREC + (m + 1) * wide],
            (((0,), (0,)), ((), ())),
            preferred_element_type=F32,
        )
        first = (PREC + m * wide) // LANES
        column = jnp.concatenate(
            [stats_t[LANES // 2 + first + i : LANES // 2 + first + i + 1] for i in range(wide // LANES)], axis=1
        )
        row = jnp.concatenate(
            [stats[:, LANES // 2 + k : LANES // 2 + k + 1] for k in range(PREC // LANES)], axis=0
        )
        cross = cross * row * column
        cross_ref[:, m] = cross.reshape(row_shards, PREC // row_shards, wide)


def local(observed, frame_kernel, scan_kernel, prec_window, frag_window):
    frames, scans, channels = observed.shape
    row_shards, mobs = lax.axis_size("rt"), lax.axis_size("mob")
    owners = row_shards * mobs
    per_lane = LANES // frames
    quads = scans // per_lane
    rows = channels // owners * quads
    group = 8 * per_lane * mobs
    blocks = row_shards * frames // BLOCK
    out_rows = rows + 8
    width = (channels - PREC) // mobs
    vmem = pl.BlockSpec(memory_space=pltpu.VMEM)
    smem = pl.BlockSpec(memory_space=pltpu.SMEM)
    depth = 3 * BLOCK + 3 * HALO
    radii = ((frame_kernel.shape[0] - 1) // 2, (scan_kernel.shape[0] - 1) // 2)
    packed, wf, wa, sf, sa = pl.pallas_call(
        functools.partial(pack_kernel, frames=frames, scans=scans, radii=radii, group=group),
        out_shape=(
            jax.ShapeDtypeStruct((owners * rows, LANES), F32),
            jax.ShapeDtypeStruct((depth, BLOCK), BF16),
            jax.ShapeDtypeStruct((depth, BLOCK), BF16),
            jax.ShapeDtypeStruct((group, 3 * group), BF16),
            jax.ShapeDtypeStruct((group, 3 * group), BF16),
        ),
        in_specs=[smem, smem, vmem],
        out_specs=[vmem] * 5,
        name="pack",
    )(frame_kernel, scan_kernel, to_tiles(observed))
    arrived = lax.all_to_all(packed.reshape(owners, rows, LANES), AXES, 0, 0, tiled=True)
    deblurred = pl.pallas_call(
        functools.partial(
            deblur_kernel, frames=frames, mobs=mobs, rows=rows, cells=frames * scans * owners
        ),
        out_shape=jax.ShapeDtypeStruct((owners * out_rows, LANES), F32),
        in_specs=[vmem] * 5,
        out_specs=vmem,
        scratch_shapes=[
            pltpu.VMEM((blocks, group, BLOCK), F32),
            pltpu.VMEM((blocks, group, BLOCK), F32),
            pltpu.VMEM((8, LANES), F32),
        ],
        name="deblur",
    )(arrived.reshape(owners * rows, LANES), wf, wa, sf, sa)
    returned = lax.all_to_all(deblurred.reshape(owners, out_rows, LANES), AXES, 0, 0, tiled=True)
    estimate, cross = pl.pallas_call(
        functools.partial(
            unpack_kernel, frames=frames, scans=scans, rows=rows, shards=(row_shards, mobs)
        ),
        out_shape=(
            jax.ShapeDtypeStruct((frames * scans * channels // LANES, LANES), F32),
            jax.ShapeDtypeStruct((row_shards, mobs, PREC // row_shards, width), F32),
        ),
        in_specs=[vmem],
        out_specs=[vmem] * 2,
        scratch_shapes=[pltpu.VMEM((frames * scans, channels), BF16)],
        name="unpack",
    )(returned.reshape(owners * out_rows, LANES))
    sums = lax.all_to_all(cross.reshape(owners, PREC // row_shards, width), AXES, 0, 0, tiled=True)
    pair_mask = (prec_window[:, None] == frag_window[None, :]).astype(F32)
    correlation = pair_mask * jnp.sum(sums, axis=0)
    return from_tiles(estimate, frames, scans), correlation


def solution(mesh):
    placed = (P("rt", "mob", None), P(), P(), P("rt"), P("mob"))
    return jax.shard_map(
        local,
        mesh=mesh,
        in_specs=placed,
        out_specs=(P("rt", "mob", None), P("rt", "mob")),
        check_vma=False,
    )
```

time: 735 us -> 159 us (0.22)
  other arithmetic: 264 us -> 0.81 us
  waiting for transfers between devices: 249 us -> 0 us
  starting transfers between devices: 42.8 us -> 0 us
  Pallas kernels: 0 us -> 38.7 us
  local copies, waits for them, and re-layouts: 21.7 us -> 0.01 us
  blocking collectives: 139 us -> 119 us
  between operations: 14.5 us -> 0.65 us
    psum x2 -> x0, blocking collectives: 139 us -> none  [the longest x1 74.5 us: local(): channel_total = lax.psum(jnp.sum(profiles, axis=0), ('rt', 'mob'))]
    add x4 -> x0, other arithmetic: 138 us -> none  [apply_taps(): running + kernel[tap_index] * lax.slice_in_dim(padded, tap_index, tap_ind...]
    ppermute x16 -> x0, waiting for transfers between devices: 130 us -> none  [the longest x8 89.9 us: extended(): lax.ppermute(tail, axis, [(i, (i + 1) % count) for i in range(ends)])]
    reduce_scatter x2 -> x0, waiting for transfers between devices: 119 us -> none  [the longest x1 69 us: local(): lax.psum_scatter(cross_sums, 'rt', scatter_dimension=0, tiled=True)]
    all_to_all x0 -> x3, blocking collectives: none -> 119 us  [the longest x1 47.2 us: local(): lax.all_to_all(packed.reshape(owners, rows, LANES), AXES, 0, 0, tiled=True)]
    div x3 -> x0, other arithmetic: 88.8 us -> none  [the longest x2 88.8 us: local(): ratio_field = observed / blurred_image]
    ppermute x16 -> x0, starting transfers between devices: 42.7 us -> none  [the longest x8 28.6 us: extended(): lax.ppermute(tail, axis, [(i, (i + 1) % count) for i in range(ends)])]
    pallas_call x0 -> x3, Pallas kernels: none -> 38.7 us  [the longest x1 25.3 us: local(): pl.pallas_call(functools.partial(deblur_kernel, frames=frames, mobs=mobs,...]
  transfers between devices with their start and end apart: 18 -> 0, of which waited for: 18 -> 0; matrix products, arithmetic and copies ran while one was open for 1% -> 0% of each run, Pallas kernels for 0% -> 0%
where the time goes in v1:
time: 159 us
  blocking collectives  119 us (75%)
  Pallas kernels  38.7 us (24%)
    all_to_all x1, blocking collectives, local(): lax.all_to_all(packed.reshape(owners, rows, LANES), AXES, 0, 0, tiled=True)  47.2 us
    all_to_all x1, blocking collectives, local(): lax.all_to_all(deblurred.reshape(owners, out_rows, LANES), AXES, 0, 0, ti...  46 us
    all_to_all x1, blocking collectives, local(): lax.all_to_all(cross.reshape(owners, PREC // row_shards, width), AXES, 0,...  25.6 us
    pallas_call x1, Pallas kernels, local(): pl.pallas_call(functools.partial(deblur_kernel, frames=frames, mobs=mobs,...  25.3 us
    pallas_call x1, Pallas kernels, local(): pl.pallas_call(functools.partial(pack_kernel, frames=frames, scans=scans,...  6.99 us
    pallas_call x1, Pallas kernels, local(): pl.pallas_call(functools.partial(unpack_kernel, frames=frames, scans=scan...  6.48 us

profile of v1, /device:TPU:1, one launch (start us, length us, event | category | flops | bytes accessed | tf_op | source)
XLA Modules:
  0.0 159.0 jit_solution(397181312734666075)
XLA Ops:
  0.6 7.0 %pack.1 = (f32[5120,128]{1,0:T(8,128)}, bf16[1152,256]{1,0:T(8,128)(2,1)}, bf16[1152,256]{1,0:T(8,128)(2,1)}, bf16[128,384]{1,0:T(8,128)(2,1)}, bf16[128,384]{1,0:T(8,128)(2,1)}) custom-call(f32[31]{0:T(128)} %frame_ref.1, f32[15]{0:T(128)} %scan_ref.1, f32[5120,128]{1,0:T(8,128)} %bitcast.18), custom_call_target="tpu_custom_call" | custom-call | tf_op jit(solution)/shard_map/pack/pallas_call | solution.py:281
  7.6 47.2 %all_to_all.15 = f32[128,40,128]{2,1,0:T(8,128)} all-to-all(f32[128,40,128]{2,1,0:T(8,128)} %bitcast.19), channel_id=1, replica_groups=mesh['rt'=32,'mob'=4] {'rt','mob'}, dimensions={0} | all-to-all | bytes 5242880 | tf_op jit(solution)/shard_map/all_to_all | solution.py:294
  54.8 25.3 %deblur.1 = f32[6144,128]{1,0:T(8,128)} custom-call(f32[5120,128]{1,0:T(8,128)} %bitcast.17, bf16[1152,256]{1,0:T(8,128)(2,1)} %get-tuple-element.10.wf_ref, bf16[1152,256]{1,0:T(8,128)(2,1)} %get-tuple-element.11.wa_ref, bf16[128,384]{1,0:T(8,128)(2,1)} %get-tuple-element.12.sf_ref, bf16[128,384]{1,0:T(8,128)(2,1)} %get-tuple-element.13.sa_ref), custom_call_target="tpu_custom_call" | custom-call | tf_op jit(solution)/shard_map/deblur/pallas_call | solution.py:295
  80.1 46.0 %all_to_all.16 = f32[128,48,128]{2,1,0:T(8,128)} all-to-all(f32[128,48,128]{2,1,0:T(8,128)} %bitcast.15), channel_id=1, replica_groups=mesh['rt'=32,'mob'=4] {'rt','mob'}, dimensions={0} | all-to-all | bytes 6291456 | tf_op jit(solution)/shard_map/all_to_all | solution.py:309
  126.1 0.0 copy-start
  126.1 0.0 copy-start.1
  126.1 6.5 %unpack.1 = (f32[5120,128]{1,0:T(8,128)}, f32[32,4,8,256]{3,2,1,0:T(8,128)}) custom-call(f32[6144,128]{1,0:T(8,128)} %bitcast.16), custom_call_target="tpu_custom_call" | custom-call | tf_op jit(solution)/shard_map/unpack/pallas_call | solution.py:310
  132.6 25.6 %all_to_all.17 = f32[128,8,256]{2,1,0:T(8,128)S(1)} all-to-all(f32[128,8,256]{2,1,0:T(8,128)} %bitcast.20), channel_id=1, replica_groups=mesh['rt'=32,'mob'=4] {'rt','mob'}, dimensions={0} | all-to-all | bytes 2097152 | tf_op jit(solution)/shard_map/all_to_all | solution.py:323
  158.2 0.1 reduce_sum.9
  158.3 0.0 copy-done
  158.3 0.0 copy-done.1
  158.3 0.7 compare_select_fusion
Async XLA Ops:
  126.1 32.2 %copy-start = (s32[256]{0:T(256)S(1)}, s32[256]{0:T(256)}, u32[]{:S(2)}) copy-start(s32[256]{0:T(256)} %param.9) | copy-start | bytes 3076
  126.1 32.2 %copy-start.1 = (s32[8]{0:T(128)S(1)}, s32[8]{0:T(128)}, u32[]{:S(2)}) copy-start(s32[8]{0:T(128)} %param.8) | copy-start | bytes 100

commit v2 on v1

--- a/solution.py
+++ b/solution.py
@@ -12,6 +12,7 @@
 LANES = 128
 AXES = ("rt", "mob")
 BLOCK = 256
+STATS = 2
 HALO = 128
 
 F32 = jnp.float32
@@ -46,9 +47,7 @@
     return field.reshape(frames, scans, tiles * LANES)
 
 
-def pack_kernel(
-    frame_ref, scan_ref, x_ref, p_ref, wf_ref, wa_ref, sf_ref, sa_ref, *, frames, scans, radii, group
-):
+def pack_kernel(x_ref, p_ref, *, frames, scans):
     per_lane = LANES // frames
     quads = scans // per_lane
     owners = LANES
@@ -65,7 +64,11 @@
 
     lax.fori_loop(0, tiles, body, 0)
 
-    frame_radius, scan_radius = radii
+
+def bands_kernel(frame_ref, scan_ref, wf_ref, wa_ref, sf_ref, sa_ref, *, scans, per_lane):
+    frame_radius, scan_radius = (frame_ref.shape[0] - 1) // 2, (scan_ref.shape[0] - 1) // 2
+    quads = scans // per_lane
+    group = sf_ref.shape[0]
     source = lax.broadcasted_iota(jnp.int32, (BLOCK, BLOCK), 0)
     target = lax.broadcasted_iota(jnp.int32, (BLOCK, BLOCK), 1)
     edge = lax.broadcasted_iota(jnp.int32, (HALO, BLOCK), 0)
@@ -175,7 +178,7 @@
     def body(pair, carry):
         def at(run, y, mob, stride):
             start = ((run * per_lane + y) * mobs + mob) * stride + pair * 8
-            return pl.ds(pl.multiple_of(start, 8), 8)
+            return pl.ds(pl.multiple_of(start, 8) if stride % 8 == 0 else start, 8)
 
         for run in range(blocks * halves):
             n, half = run // halves, run % halves
@@ -224,43 +227,50 @@
 
     lax.fori_loop(0, rows // 8, body, 0)
     for owner in range(owners):
-        out_ref[owner * out_rows + rows : owner * out_rows + rows + 8, :] = mean_ref[...]
-
-
-def unpack_kernel(q_ref, est_ref, cross_ref, centered_ref, *, frames, scans, rows, shards):
+        out_ref[owner * out_rows + rows : (owner + 1) * out_rows, :] = mean_ref[0:STATS, :]
+
+
+def cross_kernel(q_ref, cross_ref, centered_ref, *, quads):
+    owners = LANES
+    stride = q_ref.shape[0] // owners
+    channels = centered_ref.shape[0]
+    tiles = channels // LANES
+    row_shards, column_shards, shard_rows, wide = cross_ref.shape
+    stats = q_ref[pl.ds(tiles * quads, owners, stride=stride), :]
+    stats_t = stats.T
+    for k in range(tiles):
+        mean = jnp.broadcast_to(stats[:, k : k + 1], (owners, LANES))
+        for q in range(quads):
+            block = q_ref[pl.ds(k * quads + q, owners, stride=stride), :]
+            centered_ref[k * LANES : (k + 1) * LANES, q * LANES : (q + 1) * LANES] = (block - mean).astype(BF16)
+    row = jnp.concatenate([stats[:, LANES // 2 + k : LANES // 2 + k + 1] for k in range(PREC // LANES)], axis=0)
+    for m in range(column_shards):
+        cross = lax.dot_general(
+            centered_ref[:PREC, :],
+            centered_ref[PREC + m * wide : PREC + (m + 1) * wide, :],
+            (((1,), (1,)), ((), ())),
+            preferred_element_type=F32,
+        )
+        first = LANES // 2 + (PREC + m * wide) // LANES
+        column = jnp.concatenate([stats_t[first + i : first + i + 1] for i in range(wide // LANES)], axis=1)
+        cross_ref[:, m] = (cross * row * column).reshape(row_shards, shard_rows, wide)
+
+
+def unpack_kernel(q_ref, est_ref, *, frames, scans):
     owners = LANES
     stride = q_ref.shape[0] // owners
     per_lane = LANES // frames
     quads = scans // per_lane
-    channels = centered_ref.shape[1]
-    tiles = channels // LANES
-    stats = q_ref[pl.ds(rows, owners, stride=stride), :]
-    stats_t = stats.T
-    for k in range(channels // LANES):
-        lanes = slice(k * LANES, (k + 1) * LANES)
+    tiles = est_ref.shape[0] // (frames * scans)
+
+    def body(k, carry):
         for q in range(quads):
             block = q_ref[pl.ds(k * quads + q, owners, stride=stride), :].T
             for j in range(per_lane):
                 est_ref[frame_rows(q * per_lane + j, k, frames, scans, tiles), :] = block[j * frames : (j + 1) * frames]
-            centered_ref[q * LANES : (q + 1) * LANES, lanes] = (block - stats_t[k : k + 1]).astype(BF16)
-    row_shards, column_shards = shards
-    wide = (channels - PREC) // column_shards
-    for m in range(column_shards):
-        cross = lax.dot_general(
-            centered_ref[:, :PREC],
-            centered_ref[:, PREC + m * wide : PREC + (m + 1) * wide],
-            (((0,), (0,)), ((), ())),
-            preferred_element_type=F32,
-        )
-        first = (PREC + m * wide) // LANES
-        column = jnp.concatenate(
-            [stats_t[LANES // 2 + first + i : LANES // 2 + first + i + 1] for i in range(wide // LANES)], axis=1
-        )
-        row = jnp.concatenate(
-            [stats[:, LANES // 2 + k : LANES // 2 + k + 1] for k in range(PREC // LANES)], axis=0
-        )
-        cross = cross * row * column
-        cross_ref[:, m] = cross.reshape(row_shards, PREC // row_shards, wide)
+        return carry
+
+    lax.fori_loop(0, tiles, body, 0)
 
 
 def local(observed, frame_kernel, scan_kernel, prec_window, frag_window):
@@ -272,55 +282,71 @@
     rows = channels // owners * quads
     group = 8 * per_lane * mobs
     blocks = row_shards * frames // BLOCK
-    out_rows = rows + 8
+    out_rows = rows + STATS
     width = (channels - PREC) // mobs
     vmem = pl.BlockSpec(memory_space=pltpu.VMEM)
     smem = pl.BlockSpec(memory_space=pltpu.SMEM)
     depth = 3 * BLOCK + 3 * HALO
-    radii = ((frame_kernel.shape[0] - 1) // 2, (scan_kernel.shape[0] - 1) // 2)
-    packed, wf, wa, sf, sa = pl.pallas_call(
-        functools.partial(pack_kernel, frames=frames, scans=scans, radii=radii, group=group),
-        out_shape=(
-            jax.ShapeDtypeStruct((owners * rows, LANES), F32),
-            jax.ShapeDtypeStruct((depth, BLOCK), BF16),
-            jax.ShapeDtypeStruct((depth, BLOCK), BF16),
-            jax.ShapeDtypeStruct((group, 3 * group), BF16),
-            jax.ShapeDtypeStruct((group, 3 * group), BF16),
-        ),
-        in_specs=[smem, smem, vmem],
-        out_specs=[vmem] * 5,
-        name="pack",
-    )(frame_kernel, scan_kernel, to_tiles(observed))
+
+    def call(kernel, name, out_shape, specs, scratch=(), mib=16, micros=5, **statics):
+        return pl.pallas_call(
+            functools.partial(kernel, **statics),
+            out_shape=out_shape,
+            in_specs=specs,
+            out_specs=jax.tree.map(lambda _: vmem, out_shape),
+            scratch_shapes=scratch,
+            compiler_params=pltpu.CompilerParams(vmem_limit_bytes=mib << 20),
+            cost_estimate=pl.CostEstimate(
+                flops=micros * 10**9, bytes_accessed=micros * 3 * 10**6, transcendentals=0
+            ),
+            name=name,
+        )
+
+    shape = jax.ShapeDtypeStruct
+    cells = frames * scans
+    packed = call(
+        pack_kernel, "pack", shape((owners * rows, LANES), F32), [vmem], frames=frames, scans=scans
+    )(to_tiles(observed))
+    bands = call(
+        bands_kernel,
+        "bands",
+        (shape((depth, BLOCK), BF16),) * 2 + (shape((group, 3 * group), BF16),) * 2,
+        [smem, smem],
+        scans=scans,
+        per_lane=per_lane,
+    )(frame_kernel, scan_kernel)
     arrived = lax.all_to_all(packed.reshape(owners, rows, LANES), AXES, 0, 0, tiled=True)
-    deblurred = pl.pallas_call(
-        functools.partial(
-            deblur_kernel, frames=frames, mobs=mobs, rows=rows, cells=frames * scans * owners
-        ),
-        out_shape=jax.ShapeDtypeStruct((owners * out_rows, LANES), F32),
-        in_specs=[vmem] * 5,
-        out_specs=vmem,
-        scratch_shapes=[
+    deblurred = call(
+        deblur_kernel,
+        "deblur",
+        shape((owners * out_rows, LANES), F32),
+        [vmem] * 5,
+        [
             pltpu.VMEM((blocks, group, BLOCK), F32),
             pltpu.VMEM((blocks, group, BLOCK), F32),
             pltpu.VMEM((8, LANES), F32),
         ],
-        name="deblur",
-    )(arrived.reshape(owners * rows, LANES), wf, wa, sf, sa)
-    returned = lax.all_to_all(deblurred.reshape(owners, out_rows, LANES), AXES, 0, 0, tiled=True)
-    estimate, cross = pl.pallas_call(
-        functools.partial(
-            unpack_kernel, frames=frames, scans=scans, rows=rows, shards=(row_shards, mobs)
-        ),
-        out_shape=(
-            jax.ShapeDtypeStruct((frames * scans * channels // LANES, LANES), F32),
-            jax.ShapeDtypeStruct((row_shards, mobs, PREC // row_shards, width), F32),
-        ),
-        in_specs=[vmem],
-        out_specs=[vmem] * 2,
-        scratch_shapes=[pltpu.VMEM((frames * scans, channels), BF16)],
-        name="unpack",
-    )(returned.reshape(owners * out_rows, LANES))
+        mib=24,
+        frames=frames,
+        mobs=mobs,
+        rows=rows,
+        cells=cells * owners,
+    )(arrived.reshape(owners * rows, LANES), *bands)
+    returned = lax.all_to_all(
+        deblurred.reshape(owners, out_rows // STATS, STATS, LANES), AXES, 0, 0, tiled=True
+    ).reshape(owners * out_rows, LANES)
+    cross = call(
+        cross_kernel,
+        "cross",
+        shape((row_shards, mobs, PREC // row_shards, width), F32),
+        [vmem],
+        [pltpu.VMEM((channels, cells), BF16)],
+        quads=quads,
+    )(returned)
     sums = lax.all_to_all(cross.reshape(owners, PREC // row_shards, width), AXES, 0, 0, tiled=True)
+    estimate = call(
+        unpack_kernel, "unpack", shape((cells * channels // LANES, LANES), F32), [vmem], frames=frames, scans=scans
+    )(returned)
     pair_mask = (prec_window[:, None] == frag_window[None, :]).astype(F32)
     correlation = pair_mask * jnp.sum(sums, axis=0)
     return from_tiles(estimate, frames, scans), correlation

time: 159 us -> 146 us (0.918)
  blocking collectives: 119 us -> 41.7 us
  waiting for transfers between devices: 0 us -> 47.8 us
  starting transfers between devices: 0 us -> 17.1 us
  Pallas kernels: 38.7 us -> 30.2 us
  local copies, waits for them, and re-layouts: 0.01 us -> 6.09 us
    all_to_all x3 -> x1, blocking collectives: 119 us -> 41.7 us  [local(): lax.all_to_all(deblurred.reshape(owners, out_rows // STATS, STATS, LANES)...]
    all_to_all x0 -> x2, waiting for transfers between devices: none -> 47.8 us  [the longest x1 32.8 us: local(): lax.all_to_all(packed.reshape(owners, rows, LANES), AXES, 0, 0, tiled=True)]
    all_to_all x0 -> x2, starting transfers between devices: none -> 17.1 us  [the longest x1 11.5 us: local(): lax.all_to_all(packed.reshape(owners, rows, LANES), AXES, 0, 0, tiled=True)]
    pallas_call x3 -> x5, Pallas kernels: 38.7 us -> 30.2 us  [the longest x1 21.5 us: local(): call(deblur_kernel, 'deblur', shape((owners * out_rows, LANES), F32), [vm...]
    unnamed x4 -> x18, local copies, waits for them, and re-layouts: 0.01 us -> 6.09 us
  transfers between devices with their start and end apart: 0 -> 2, of which waited for: 0 -> 2; matrix products, arithmetic and copies ran while one was open for 0% -> 0% of each run, Pallas kernels for 0% -> 4%
where the time goes in v2:
time: 146 us
  waiting for transfers between devices  47.8 us (33%)
  blocking collectives  41.7 us (29%)
  Pallas kernels  30.2 us (21%)
  starting transfers between devices  17.1 us (12%)
  local copies, waits for them, and re-layouts  6.09 us (4%)
  other arithmetic  2.03 us (1%)
    all_to_all x1, blocking collectives, local(): lax.all_to_all(deblurred.reshape(owners, out_rows // STATS, STATS, LANES)...  41.7 us
    all_to_all x1, waiting for transfers between devices, local(): lax.all_to_all(packed.reshape(owners, rows, LANES), AXES, 0, 0, tiled=True)  32.8 us
    pallas_call x1, Pallas kernels, local(): call(deblur_kernel, 'deblur', shape((owners * out_rows, LANES), F32), [vm...  21.5 us
    all_to_all x1, waiting for transfers between devices, local(): lax.all_to_all(cross.reshape(owners, PREC // row_shards, width), AXES, 0,...  15 us
    all_to_all x1, starting transfers between devices, local(): lax.all_to_all(packed.reshape(owners, rows, LANES), AXES, 0, 0, tiled=True)  11.5 us
    unnamed x18, local copies, waits for them, and re-layouts  6.09 us
    all_to_all x1, starting transfers between devices, local(): lax.all_to_all(cross.reshape(owners, PREC // row_shards, width), AXES, 0,...  5.62 us
    pallas_call x1, Pallas kernels, local(): call(unpack_kernel, 'unpack', shape((cells * channels // LANES, LANES), F...  3.86 us
  transfers between devices with their start and end apart: 2, of which 2 were waited for; matrix products, arithmetic and copies ran while one was open for 0% of the time, Pallas kernels for 4%

profile of v2, /device:TPU:1, one launch (start us, length us, event | category | flops | bytes accessed | tf_op | source)
XLA Modules:
  0.0 145.7 jit_solution(832887345083618443)
XLA Ops:
  0.6 0.0 copy-start.2
  0.6 1.7 %copy-done.2 = f32[32,16,1280]{2,1,0:T(8,128)S(1)} copy-done((f32[32,16,1280]{2,1,0:T(8,128)S(1)}, f32[32,16,1280]{2,1,0:T(8,128)}, u32[]{:S(2)}) %copy-start.2) | copy-done | bytes 2621464
  2.4 2.2 %pack.1 = f32[5120,128]{1,0:T(8,128)S(1)} custom-call(f32[5120,128]{1,0:T(8,128)S(1)} %bitcast.21), custom_call_target="tpu_custom_call" | custom-call | flops 5000000000 | bytes 15000000 | tf_op jit(solution)/shard_map/pack/pallas_call | solution.py:307
  4.6 1.5 %copy-done = f32[5120,128]{1,0:T(8,128)} copy-done((f32[5120,128]{1,0:T(8,128)}, f32[5120,128]{1,0:T(8,128)S(1)}, u32[]{:S(2)}) %copy-start) | copy-done | bytes 2621464
  6.1 11.5 %all-to-all-start = ((f32[128,40,128]{2,1,0:T(8,128)}), f32[128,40,128]{2,1,0:T(8,128)S(1)}, u32[]{:S(2)}, u32[]{:S(2)}) async-start(f32[128,40,128]{2,1,0:T(8,128)} %bitcast.19), calls=%async_computation | async-start | bytes 5242880 | tf_op jit(solution)/shard_map/all_to_all | solution.py:318
  17.5 0.0 copy-done.3
  17.6 0.0 copy-done.4
  17.6 2.0 %bands.1 = (bf16[1152,256]{1,0:T(8,128)(2,1)S(1)}, bf16[1152,256]{1,0:T(8,128)(2,1)S(1)}, bf16[128,384]{1,0:T(8,128)(2,1)S(1)}, bf16[128,384]{1,0:T(8,128)(2,1)S(1)}) custom-call(f32[31]{0:T(128)S(1)} %copy-done.3, f32[15]{0:T(128)S(1)} %copy-done.4), custom_call_target="tpu_custom_call" | custom-call | flops 5000000000 | bytes 15000000 | tf_op jit(solution)/shard_map/bands/pallas_call | solution.py:310
  19.6 0.8 copy-done.5
  20.4 32.8 %all-to-all-done = f32[128,40,128]{2,1,0:T(8,128)S(1)} async-done(((f32[128,40,128]{2,1,0:T(8,128)}), f32[128,40,128]{2,1,0:T(8,128)S(1)}, u32[]{:S(2)}, u32[]{:S(2)}) %all-to-all-start) | async-done | bytes 2621472 | tf_op jit(solution)/shard_map/all_to_all | solution.py:318
  53.2 1.1 copy-done.6
  54.2 21.5 %deblur.1 = f32[5376,128]{1,0:T(8,128)S(1)} custom-call(f32[5120,128]{1,0:T(8,128)S(1)} %bitcast.18, bf16[1152,256]{1,0:T(8,128)(2,1)S(1)} %get-tuple-element.6.wf_ref, bf16[1152,256]{1,0:T(8,128)(2,1)S(1)} %copy-done.6, bf16[128,384]{1,0:T(8,128)(2,1)S(1)} %get-tuple-element.8.sf_ref, bf16[128,384]{1,0:T(8,128)(2,1)S(1)} %get-tuple-element.9.sa_ref), custom_call_target="tpu_custom_call" | custom-call | flops 5000000000 | bytes 15000000 | tf_op jit(solution)/shard_map/deblur/pallas_call | solution.py:319
  75.8 41.7 %all_to_all.15 = f32[128,21,2,128]{3,2,1,0:T(2,128)S(1)} all-to-all(f32[128,21,2,128]{3,2,1,0:T(2,128)S(1)} %bitcast.17), channel_id=1, replica_groups=mesh['rt'=32,'mob'=4] {'rt','mob'}, dimensions={0} | all-to-all | bytes 5505024 | tf_op jit(solution)/shard_map/all_to_all | solution.py:335
  117.5 0.6 cross.1
  118.1 0.0 copy-start.1
  118.1 1.0 copy-done.1
  119.1 5.6 %all-to-all-start.2 = ((f32[128,8,256]{2,1,0:T(8,128)}), f32[128,8,256]{2,1,0:T(8,128)}, u32[]{:S(2)}, u32[]{:S(2)}) async-start(f32[128,8,256]{2,1,0:T(8,128)} %bitcast.20), calls=%async_computation.2 | async-start | bytes 2097152 | tf_op jit(solution)/shard_map/all_to_all | solution.py:346
  124.8 0.0 copy-start.7
  124.8 0.0 copy-start.8
  124.8 3.9 %unpack.1 = f32[5120,128]{1,0:T(8,128)} custom-call(f32[5376,128]{1,0:T(8,128)S(1)} %bitcast.16), custom_call_target="tpu_custom_call" | custom-call | flops 5000000000 | bytes 15000000 | tf_op jit(solution)/shard_map/unpack/pallas_call | solution.py:347
  128.6 15.0 %all-to-all-done.2 = f32[128,8,256]{2,1,0:T(8,128)} async-done(((f32[128,8,256]{2,1,0:T(8,128)}), f32[128,8,256]{2,1,0:T(8,128)}, u32[]{:S(2)}, u32[]{:S(2)}) %all-to-all-start.2) | async-done | bytes 1048608 | tf_op jit(solution)/shard_map/all_to_all | solution.py:346
  143.6 1.4 reduce_sum.9
  145.0 0.0 copy-done.7
  145.0 0.7 compare_select_fusion
  (6 shorter events, 0.0 us)
Async XLA Ops:
  0.6 1.7 %copy-start.2 = (f32[32,16,1280]{2,1,0:T(8,128)S(1)}, f32[32,16,1280]{2,1,0:T(8,128)}, u32[]{:S(2)}) copy-start(f32[32,16,1280]{2,1,0:T(8,128)} %param.5) | copy-start | bytes 7864324
  4.6 1.5 %copy-start = (f32[5120,128]{1,0:T(8,128)}, f32[5120,128]{1,0:T(8,128)S(1)}, u32[]{:S(2)}) copy-start(f32[5120,128]{1,0:T(8,128)S(1)} %pack.1) | copy-start | bytes 7864324
  6.1 11.5 %copy-start.3 = (f32[31]{0:T(128)S(1)}, f32[31]{0:T(128)}, u32[]{:S(2)}) copy-start(f32[31]{0:T(128)} %frame_ref.1) | copy-start | bytes 376
  6.1 11.5 %copy-start.4 = (f32[15]{0:T(128)S(1)}, f32[15]{0:T(128)}, u32[]{:S(2)}) copy-start(f32[15]{0:T(128)} %scan_ref.1) | copy-start | bytes 184
  6.1 47.1 %all-to-all-start = ((f32[128,40,128]{2,1,0:T(8,128)}), f32[128,40,128]{2,1,0:T(8,128)S(1)}, u32[]{:S(2)}, u32[]{:S(2)}) async-start(f32[128,40,128]{2,1,0:T(8,128)} %bitcast.19), calls=%async_computation | async-start | bytes 5242880 | tf_op jit(solution)/shard_map/all_to_all | solution.py:318
  19.6 0.8 copy-start.5
  53.2 1.1 copy-start.6
  118.1 1.0 copy-start.1
  119.1 24.5 %all-to-all-start.2 = ((f32[128,8,256]{2,1,0:T(8,128)}), f32[128,8,256]{2,1,0:T(8,128)}, u32[]{:S(2)}, u32[]{:S(2)}) async-start(f32[128,8,256]{2,1,0:T(8,128)} %bitcast.20), calls=%async_computation.2 | async-start | bytes 2097152 | tf_op jit(solution)/shard_map/all_to_all | solution.py:346
  124.8 20.3 %copy-start.7 = (s32[256]{0:T(256)S(1)}, s32[256]{0:T(256)}, u32[]{:S(2)}) copy-start(s32[256]{0:T(256)} %param.9) | copy-start | bytes 3076
  124.8 20.2 %copy-start.8 = (s32[8]{0:T(128)S(1)}, s32[8]{0:T(128)}, u32[]{:S(2)}) copy-start(s32[8]{0:T(128)} %param.8) | copy-start | bytes 100

commit v3 on v2

v3 whole, which is shorter than its diff:
```python
import functools

import jax
import jax.numpy as jnp
from jax import lax
from jax.experimental import pallas as pl
from jax.experimental.pallas import tpu as pltpu
from jax.sharding import PartitionSpec as P

PREC = 256
ITERS = 2
LANES = 128
AXES = ("rt", "mob")
BLOCK = 256
EDGE = 16
TOGETHER = 2
STATS = 2
HALO = 128

F32 = jnp.float32
BF16 = jnp.bfloat16


def split(values):
    high = values.astype(BF16)
    return high, (values - high.astype(F32)).astype(BF16)


def taps_at(offset, taps_ref, count):
    out = jnp.zeros(offset.shape, F32)
    for tap in range(count):
        out = jnp.where(offset == tap, taps_ref[tap], out)
    return out


def frame_rows(scan, k, frames, scans, tiles):
    return pl.ds((scan // 8 * tiles + k) * 8 + scan % 8, frames, stride=scans * tiles)


def to_tiles(field):
    frames, scans, channels = field.shape
    field = field.reshape(frames, scans // 8, 8, channels // LANES, LANES).transpose(0, 1, 3, 2, 4)
    return field.reshape(frames * scans // 8, channels // LANES, 8, LANES)


def from_tiles(rows, frames, scans):
    tiles = rows.shape[0] // (frames * scans)
    field = rows.reshape(frames, scans // 8, tiles, 8, LANES).transpose(0, 1, 3, 2, 4)
    return field.reshape(frames, scans, tiles * LANES)


def pack_kernel(x_hbm, p_hbm, x_ref, p_ref, in_sem, out_sem, *, frames, scans):
    per_lane = LANES // frames
    quads = scans // per_lane
    owners, rows = LANES, p_ref.shape[0] // LANES
    tiles = x_ref.shape[0]
    steps = rows // 8
    each = tiles // steps

    def arrive(k):
        return pltpu.make_async_copy(x_hbm.at[:, k], x_ref.at[k], in_sem.at[k])

    def leave(step):
        here = pl.ds(pl.multiple_of(step * 8, 8), 8)
        return pltpu.make_async_copy(
            p_ref.reshape(owners, rows, LANES).at[:, here], p_hbm.at[:, here], out_sem.at[step]
        )

    for k in range(tiles):
        arrive(k).start()

    def body(step, carry):
        for sub in range(each):
            k = step * each + sub
            arrive(k).wait()
            view = x_ref.at[k].reshape(frames * scans, LANES)
            for q in range(quads):
                block = jnp.concatenate(
                    [view[pl.ds(q * per_lane + j, frames, stride=scans), :] for j in range(per_lane)], axis=0
                )
                p_ref[pl.ds(k * quads + q, owners, stride=rows), :] = block.T
        leave(step).start()
        return carry

    lax.fori_loop(0, steps, body, 0)
    for step in range(steps):
        leave(step).wait()


def bands_kernel(frame_ref, scan_ref, wf_ref, wa_ref, sf_ref, sa_ref, *, scans, per_lane):
    frame_radius, scan_radius = (frame_ref.shape[0] - 1) // 2, (scan_ref.shape[0] - 1) // 2
    quads = scans // per_lane
    group = sf_ref.shape[0] // 2
    source = lax.broadcasted_iota(jnp.int32, (BLOCK, BLOCK), 0)
    target = lax.broadcasted_iota(jnp.int32, (BLOCK, BLOCK), 1)
    edge_row = lax.broadcasted_iota(jnp.int32, (HALO, BLOCK), 0)
    edge = jnp.where(edge_row < HALO // 2, edge_row + BLOCK, edge_row - HALO)
    again = (edge_row >= EDGE) & (edge_row < 3 * EDGE)
    edge_again = jnp.where(edge_row < 2 * EDGE, edge_row - 2 * EDGE, edge_row - 2 * EDGE + BLOCK)
    edge_target = lax.broadcasted_iota(jnp.int32, (HALO, BLOCK), 1)
    for ref, sign in ((wf_ref, 1), (wa_ref, -1)):
        high, low = split(taps_at(sign * (source - target) + frame_radius, frame_ref, 2 * frame_radius + 1))
        edge_high, _ = split(
            taps_at(sign * (edge - edge_target) + frame_radius, frame_ref, 2 * frame_radius + 1)
        )
        _, edge_low = split(
            taps_at(sign * (edge_again - edge_target) + frame_radius, frame_ref, 2 * frame_radius + 1)
        )
        pieces = (high, high, low, jnp.where(again, edge_low, edge_high), edge_high)
        at = 0
        for piece in pieces:
            ref[at : at + piece.shape[0], :] = piece
            at += piece.shape[0]
    row = lax.broadcasted_iota(jnp.int32, (group, group), 0)
    col = lax.broadcasted_iota(jnp.int32, (group, group), 1)

    def place(index):
        tile, inner = index // 8, index % 8
        scan = (tile // per_lane) * scans + (inner % quads) * per_lane + tile % per_lane
        return scan, inner // quads

    row_scan, row_channel = place(row)
    col_scan, col_channel = place(col)
    for ref, sign in ((sf_ref, 1), (sa_ref, -1)):
        matrix = jnp.where(
            row_channel == col_channel,
            taps_at(sign * (col_scan - row_scan) + scan_radius, scan_ref, 2 * scan_radius + 1),
            0.0,
        )
        high, low = split(matrix)
        ref[0:group, 0:group] = high
        ref[0:group, group : 2 * group] = high
        ref[group : 2 * group, 0:group] = low
        ref[group : 2 * group, group : 2 * group] = jnp.zeros_like(low)


def swap_blocks(tiles, lane, width):
    first, second, third, fourth = tiles
    wide = lane < 2 * width
    narrow = (lane % (2 * width)) < width
    pairs = []
    for a, b in ((first, third), (second, fourth)):
        pairs.append(
            (
                jnp.where(wide, a, pltpu.roll(b, 2 * width, 1)),
                jnp.where(wide, pltpu.roll(a, 2 * width, 1), b),
            )
        )
    out = []
    for a, b in zip(pairs[0], pairs[1]):
        out.append(jnp.where(narrow, a, pltpu.roll(b, width, 1)))
        out.append(jnp.where(narrow, pltpu.roll(a, LANES - width, 1), b))
    return out


def deblur_kernel(
    p_ref, wf_hbm, wa_hbm, sf_hbm, sa_hbm, out_ref,
    wf_ref, wa_ref, sf_ref, sa_ref, obs_ref, est_ref, left_ref, back_ref, mean_ref, band_sem,
    *, frames, mobs, rows, cells,
):
    copies = [
        pltpu.make_async_copy(source, target, band_sem.at[i])
        for i, (source, target) in enumerate(
            ((sf_hbm, sf_ref), (wf_hbm, wf_ref), (wa_hbm, wa_ref), (sa_hbm, sa_ref))
        )
    ]
    for copy in copies:
        copy.start()
    owners = LANES
    out_rows = out_ref.shape[0] // owners
    units, blocks, group, width = obs_ref.shape
    per_lane = LANES // frames
    lane = lax.broadcasted_iota(jnp.int32, (8, LANES), 1)
    row8 = lax.broadcasted_iota(jnp.int32, (8, 1), 0)
    halo_lane = lax.broadcasted_iota(jnp.int32, (group, HALO), 1)
    halves = width // LANES

    def at(pair, run, y, mob, stride):
        start = ((run * per_lane + y) * mobs + mob) * stride + pair * 8
        return pl.ds(start, 8)

    def scan_blur(values, matrix):
        high, low = split(values)
        both = jnp.dot(matrix, jnp.concatenate([high, low], axis=0), preferred_element_type=F32)
        return both[0:group] + both[group : 2 * group]

    def put(ref, u, n, values):
        high, low = split(values)
        ref[u, n * group : (n + 1) * group, 0:width] = high
        ref[u, n * group : (n + 1) * group, width : 2 * width] = low

    def put_halo(ref, u):
        zero = jnp.zeros((group, HALO), BF16)
        for n in range(blocks):
            here = slice(n * group, (n + 1) * group)
            for which in (0, 1):
                first = which * width
                after = before = zero
                if n + 1 < blocks:
                    after = ref[u, (n + 1) * group : (n + 2) * group, first : first + HALO]
                if n:
                    before = ref[u, (n - 1) * group : n * group, first + width - HALO : first + width]
                halo = jnp.where(halo_lane < HALO // 2, after, before)
                if which == 0:
                    again = (halo_lane >= EDGE) & (halo_lane < 3 * EDGE)
                    halo = jnp.where(again, pltpu.roll(halo, 2 * EDGE, 1), halo)
                ref[u, here, 2 * width + which * HALO : 2 * width + (which + 1) * HALO] = halo

    def frame_blur(ref, members, matrix):
        lhs = []
        for u in members:
            center, rest = ref[u, :, 0 : 2 * width], ref[u, :, 2 * width : 2 * width + 2 * HALO]
            lhs.append(jnp.concatenate([center, center[:, 0:width], rest], axis=1))
        out = jnp.dot(jnp.concatenate(lhs, axis=0), matrix, preferred_element_type=F32)
        return {
            u: [out[(k * blocks + n) * group : (k * blocks + n + 1) * group] for n in range(blocks)]
            for k, u in enumerate(members)
        }

    def total8(parts):
        acc = None
        for part in parts:
            for half in range(halves):
                piece = part[:, half * LANES : (half + 1) * LANES].reshape(group // 8, 8, LANES).sum(axis=0)
                acc = piece if acc is None else acc + piece
        rows_sum = jnp.sum(acc, axis=1, keepdims=True)
        zero = jnp.zeros_like(rows_sum)
        upper = jnp.sum(jnp.where(row8 < 4, rows_sum, zero), axis=0, keepdims=True)
        lower = jnp.sum(jnp.where(row8 < 4, zero, rows_sum), axis=0, keepdims=True)
        return upper, lower

    def gather(u, pair):
        for run in range(blocks * halves):
            n, half = run // halves, run % halves
            for mob in range(mobs):
                tiles = [p_ref[at(pair, run, y, mob, rows), :] for y in range(per_lane)]
                for j, tile in enumerate(swap_blocks(tiles, lane, frames)):
                    b = mob * per_lane + j
                    obs_ref[u, n, b * 8 : b * 8 + 8, half * LANES : (half + 1) * LANES] = tile

    def scatter(u, pair):
        for run in range(blocks * halves):
            n, half = run // halves, run % halves
            for mob in range(mobs):
                tiles = []
                for j in range(per_lane):
                    b = mob * per_lane + j
                    tiles.append(est_ref[u, n, b * 8 : b * 8 + 8, half * LANES : (half + 1) * LANES])
                for y, tile in enumerate(swap_blocks(tiles, lane, frames)):
                    out_ref[at(pair, run, y, mob, out_rows), :] = tile

    def forward(u, iteration):
        estimate = obs_ref if iteration == 0 else est_ref
        for n in range(blocks):
            put(left_ref, u, n, scan_blur(estimate[u, n], sf_ref[...]))
        put_halo(left_ref, u)

    def ratios(u, done):
        for n, blurred in enumerate(done[u]):
            put(back_ref, u, n, obs_ref[u, n] / blurred)
        put_halo(back_ref, u)

    def adjoint(u, iteration, done):
        estimate = obs_ref if iteration == 0 else est_ref
        for n, blurred in enumerate(done[u]):
            est_ref[u, n] = estimate[u, n] * scan_blur(blurred, sa_ref[...])

    def statistics(u, pair):
        upper, lower = total8([est_ref[u, n] for n in range(blocks)])
        upper_mean, lower_mean = upper / cells, lower / cells
        mean8 = jnp.where(row8 < 4, upper_mean, lower_mean)
        squares = []
        for n in range(blocks):
            centered = est_ref[u, n].reshape(group // 8, 8, width) - mean8[None]
            centered = centered.astype(BF16).astype(F32).reshape(group, width)
            squares.append(centered * centered)
        upper_sq, lower_sq = total8(squares)
        upper_inv = 1.0 / jnp.sqrt(upper_sq + 1e-06)
        lower_inv = 1.0 / jnp.sqrt(lower_sq + 1e-06)
        held = mean_ref[...]
        held = jnp.where(lane == 2 * pair, upper_mean, held)
        held = jnp.where(lane == 2 * pair + 1, lower_mean, held)
        held = jnp.where(lane == LANES // 2 + 2 * pair, upper_inv, held)
        held = jnp.where(lane == LANES // 2 + 2 * pair + 1, lower_inv, held)
        mean_ref[...] = held

    members = range(units)
    sets = [members[first : first + TOGETHER] for first in range(0, units, TOGETHER)]
    mean_ref[...] = jnp.zeros_like(mean_ref)
    for u in members:
        gather(u, u)
    for copy in copies:
        copy.wait()
    for iteration in range(ITERS):
        for u in members:
            forward(u, iteration)
        for some in sets:
            done = frame_blur(left_ref, some, wf_ref[...])
            for u in some:
                ratios(u, done)
        for some in sets:
            done = frame_blur(back_ref, some, wa_ref[...])
            for u in some:
                adjoint(u, iteration, done)
    for u in members:
        statistics(u, u)
        scatter(u, u)
    for owner in range(owners):
        out_ref[owner * out_rows + rows : (owner + 1) * out_rows, :] = mean_ref[0:STATS, :]


def cross_kernel(q_ref, cross_hbm, centered_ref, cross_ref, out_sem, *, quads):
    owners = LANES
    stride = q_ref.shape[0] // owners
    channels = centered_ref.shape[0]
    tiles = channels // LANES
    column_shards, row_shards, shard_rows, wide = cross_ref.shape
    copies = []
    stats = q_ref[pl.ds(tiles * quads, owners, stride=stride), :]
    stats_t = stats.T
    for k in range(tiles):
        mean = jnp.broadcast_to(stats[:, k : k + 1], (owners, LANES))
        for q in range(quads):
            block = q_ref[pl.ds(k * quads + q, owners, stride=stride), :]
            centered_ref[k * LANES : (k + 1) * LANES, q * LANES : (q + 1) * LANES] = (block - mean).astype(BF16)
    row = jnp.concatenate([stats[:, LANES // 2 + k : LANES // 2 + k + 1] for k in range(PREC // LANES)], axis=0)
    for m in range(column_shards):
        cross = lax.dot_general(
            centered_ref[:PREC, :],
            centered_ref[PREC + m * wide : PREC + (m + 1) * wide, :],
            (((1,), (1,)), ((), ())),
            preferred_element_type=F32,
        )
        first = LANES // 2 + (PREC + m * wide) // LANES
        column = jnp.concatenate([stats_t[first + i : first + i + 1] for i in range(wide // LANES)], axis=1)
        cross_ref[m] = (cross * row * column).reshape(row_shards, shard_rows, wide)
        copies.append(pltpu.make_async_copy(cross_ref.at[m], cross_hbm.at[:, m], out_sem.at[m]))
        copies[-1].start()
    for copy in copies:
        copy.wait()


def finish_kernel(sums_ref, mask_ref, out_ref):
    out_ref[...] = mask_ref[...] * jnp.sum(sums_ref[...], axis=0)


def unpack_kernel(q_ref, est_ref, *, frames, scans):
    owners = LANES
    stride = q_ref.shape[0] // owners
    per_lane = LANES // frames
    quads = scans // per_lane
    tiles = est_ref.shape[0] // (frames * scans)

    def body(k, carry):
        for q in range(quads):
            block = q_ref[pl.ds(k * quads + q, owners, stride=stride), :].T
            for j in range(per_lane):
                est_ref[frame_rows(q * per_lane + j, k, frames, scans, tiles), :] = block[j * frames : (j + 1) * frames]
        return carry

    lax.fori_loop(0, tiles, body, 0)


def local(observed, frame_kernel, scan_kernel, prec_window, frag_window):
    frames, scans, channels = observed.shape
    row_shards, mobs = lax.axis_size("rt"), lax.axis_size("mob")
    owners = row_shards * mobs
    per_lane = LANES // frames
    quads = scans // per_lane
    rows = channels // owners * quads
    group = 8 * per_lane * mobs
    blocks = row_shards * frames // BLOCK
    out_rows = rows + STATS
    width = (channels - PREC) // mobs
    vmem = pl.BlockSpec(memory_space=pltpu.VMEM)
    smem = pl.BlockSpec(memory_space=pltpu.SMEM)
    depth = 3 * BLOCK + 2 * HALO

    hbm = pl.BlockSpec(memory_space=pltpu.HBM)

    def call(kernel, name, out_shape, specs, scratch=(), out_spec=vmem, mib=16.0, micros=5, **statics):
        return pl.pallas_call(
            functools.partial(kernel, **statics),
            out_shape=out_shape,
            in_specs=specs,
            out_specs=jax.tree.map(lambda _: out_spec, out_shape),
            scratch_shapes=scratch,
            compiler_params=pltpu.CompilerParams(vmem_limit_bytes=int(mib * 2**20)),
            cost_estimate=pl.CostEstimate(
                flops=micros * 10**9, bytes_accessed=micros * 3 * 10**6, transcendentals=0
            ),
            name=name,
        )

    shape = jax.ShapeDtypeStruct
    cells = frames * scans
    tiles = channels // LANES
    packed = call(
        pack_kernel,
        "pack",
        shape((owners, rows, LANES), F32),
        [hbm],
        [
            pltpu.VMEM((tiles, cells // 8, 8, LANES), F32),
            pltpu.VMEM((owners * rows, LANES), F32),
            pltpu.SemaphoreType.DMA((tiles,)),
            pltpu.SemaphoreType.DMA((rows // 8,)),
        ],
        out_spec=hbm,
        mib=62,
        frames=frames,
        scans=scans,
    )(to_tiles(observed))
    bands = call(
        bands_kernel,
        "bands",
        (shape((depth, BLOCK), BF16),) * 2 + (shape((2 * group, 2 * group), BF16),) * 2,
        [smem, smem],
        mib=16,
        scans=scans,
        per_lane=per_lane,
    )(frame_kernel, scan_kernel)
    arrived = lax.all_to_all(packed, AXES, 0, 0, tiled=True)
    deblurred = call(
        deblur_kernel,
        "deblur",
        shape((owners * out_rows, LANES), F32),
        [vmem] + [hbm] * 4,
        [pltpu.VMEM(band.shape, BF16) for band in bands]
        + [
            pltpu.VMEM((rows // 8, blocks, group, BLOCK), F32),
            pltpu.VMEM((rows // 8, blocks, group, BLOCK), F32),
            pltpu.VMEM((rows // 8, blocks * group, 2 * BLOCK + 2 * HALO), BF16),
            pltpu.VMEM((rows // 8, blocks * group, 2 * BLOCK + 2 * HALO), BF16),
            pltpu.VMEM((8, LANES), F32),
            pltpu.SemaphoreType.DMA((len(bands),)),
        ],
        mib=40,
        frames=frames,
        mobs=mobs,
        rows=rows,
        cells=cells * owners,
    )(arrived.reshape(owners * rows, LANES), *bands)
    returned = lax.all_to_all(
        deblurred.reshape(owners, out_rows // STATS, STATS, LANES), AXES, 0, 0, tiled=True
    ).reshape(owners * out_rows, LANES)
    cross = call(
        cross_kernel,
        "cross",
        shape((row_shards, mobs, PREC // row_shards, width), F32),
        [vmem],
        [
            pltpu.VMEM((channels, cells), BF16),
            pltpu.VMEM((mobs, row_shards, PREC // row_shards, width), F32),
            pltpu.SemaphoreType.DMA((mobs,)),
        ],
        out_spec=hbm,
        mib=16,
        quads=quads,
    )(returned)
    sums = lax.all_to_all(cross.reshape(owners, PREC // row_shards, width), AXES, 0, 0, tiled=True)
    estimate = call(
        unpack_kernel, "unpack", shape((cells * channels // LANES, LANES), F32), [vmem], frames=frames, scans=scans
    )(returned)
    pair_mask = (prec_window[:, None] == frag_window[None, :]).astype(F32)
    correlation = call(finish_kernel, "finish", shape(pair_mask.shape, F32), [vmem] * 2)(sums, pair_mask)
    return from_tiles(estimate, frames, scans), correlation


def solution(mesh):
    placed = (P("rt", "mob", None), P(), P(), P("rt"), P("mob"))
    return jax.shard_map(
        local,
        mesh=mesh,
        in_specs=placed,
        out_specs=(P("rt", "mob", None), P("rt", "mob")),
        check_vma=False,
    )
```

time: 146 us -> 148 us (1.014)
  Pallas kernels: 30.2 us -> 37.7 us
  local copies, waits for them, and re-layouts: 6.09 us -> 2.84 us
  other arithmetic: 2.03 us -> 0.07 us
    unnamed x18 -> x14, local copies, waits for them, and re-layouts: 6.09 us -> 2.84 us
    pallas_call x1 -> x2, Pallas kernels: 2.19 us -> 5.23 us  [the longest x1 3.27 us: local(): call(pack_kernel, 'pack', shape((owners, rows, LANES), F32), [hbm], [pltp...]
    pallas_call x1, Pallas kernels: 21.5 us -> 24.5 us  [local(): call(deblur_kernel, 'deblur', shape((owners * out_rows, LANES), F32), [vm...]
where the time goes in v3:
time: 148 us; the launch traced here: 147 us
  waiting for transfers between devices  47.2 us (32%)
  blocking collectives  41.7 us (28%)
  Pallas kernels  37.7 us (25%)
  starting transfers between devices  17.1 us (12%)
  local copies, waits for them, and re-layouts  2.84 us (2%)
    all_to_all x1, blocking collectives, local(): lax.all_to_all(deblurred.reshape(owners, out_rows // STATS, STATS, LANES)...  41.7 us
    all_to_all x1, waiting for transfers between devices, local(): arrived = lax.all_to_all(packed, AXES, 0, 0, tiled=True)  32.2 us
    pallas_call x1, Pallas kernels, local(): call(deblur_kernel, 'deblur', shape((owners * out_rows, LANES), F32), [vm...  24.5 us
    all_to_all x1, waiting for transfers between devices, local(): lax.all_to_all(cross.reshape(owners, PREC // row_shards, width), AXES, 0,...  14.9 us
    all_to_all x1, starting transfers between devices, local(): arrived = lax.all_to_all(packed, AXES, 0, 0, tiled=True)  11.5 us
    all_to_all x1, starting transfers between devices, local(): lax.all_to_all(cross.reshape(owners, PREC // row_shards, width), AXES, 0,...  5.61 us
    pallas_call x1, Pallas kernels, local(): call(unpack_kernel, 'unpack', shape((cells * channels // LANES, LANES), F...  3.85 us
    pallas_call x1, Pallas kernels, local(): call(pack_kernel, 'pack', shape((owners, rows, LANES), F32), [hbm], [pltp...  3.27 us
  transfers between devices with their start and end apart: 2, of which 2 were waited for; matrix products, arithmetic and copies ran while one was open for 0% of the time, Pallas kernels for 4%

profile of v3, /device:TPU:1, one launch (start us, length us, event | category | flops | bytes accessed | tf_op | source)
XLA Modules:
  0.0 147.4 jit_solution(14642111120641670369)
XLA Ops:
  0.6 3.3 %pack.1 = f32[128,40,128]{2,1,0:T(8,128)} custom-call(f32[64,10,8,128]{3,2,1,0:T(8,128)} %bitcast.19), custom_call_target="tpu_custom_call" | custom-call | flops 5000000000 | bytes 15000000 | tf_op jit(solution)/shard_map/pack/pallas_call | solution.py:398
  3.9 0.0 copy-start.1
  3.9 0.0 copy-start.2
  3.9 11.5 %all-to-all-start = ((f32[128,40,128]{2,1,0:T(8,128)}), f32[128,40,128]{2,1,0:T(8,128)S(1)}, u32[]{:S(2)}, u32[]{:S(2)}) async-start(f32[128,40,128]{2,1,0:T(8,128)} %pack.1), calls=%async_computation | async-start | bytes 5242880 | tf_op jit(solution)/shard_map/all_to_all | solution.py:423
  15.4 0.0 copy-done.1
  15.4 0.0 copy-done.2
  15.4 2.5 %bands.1 = (bf16[1024,256]{1,0:T(8,128)(2,1)S(1)}, bf16[1024,256]{1,0:T(8,128)(2,1)S(1)}, bf16[256,256]{1,0:T(8,128)(2,1)S(1)}, bf16[256,256]{1,0:T(8,128)(2,1)S(1)}) custom-call(f32[31]{0:T(128)S(1)} %copy-done.1, f32[15]{0:T(128)S(1)} %copy-done.2), custom_call_target="tpu_custom_call" | custom-call | flops 5000000000 | bytes 15000000 | tf_op jit(solution)/shard_map/bands/pallas_call | solution.py:414
  18.0 0.0 copy-start.3
  18.0 0.8 copy-done.3
  18.8 32.2 %all-to-all-done = f32[128,40,128]{2,1,0:T(8,128)S(1)} async-done(((f32[128,40,128]{2,1,0:T(8,128)}), f32[128,40,128]{2,1,0:T(8,128)S(1)}, u32[]{:S(2)}, u32[]{:S(2)}) %all-to-all-start) | async-done | bytes 2621472 | tf_op jit(solution)/shard_map/all_to_all | solution.py:423
  51.0 0.0 copy-start.4
  51.0 1.0 copy-done.4
  52.1 24.5 %deblur.1 = f32[5376,128]{1,0:T(8,128)S(1)} custom-call(f32[5120,128]{1,0:T(8,128)S(1)} %bitcast.17, bf16[1024,256]{1,0:T(8,128)(2,1)S(1)} %get-tuple-element.6.wf_hbm, bf16[1024,256]{1,0:T(8,128)(2,1)S(1)} %copy-done.4, bf16[256,256]{1,0:T(8,128)(2,1)S(1)} %get-tuple-element.8.sf_hbm, bf16[256,256]{1,0:T(8,128)(2,1)S(1)} %get-tuple-element.9.sa_hbm), custom_call_target="tpu_custom_call" | custom-call | flops 5000000000 | bytes 15000000 | tf_op jit(solution)/shard_map/deblur/pallas_call | solution.py:424
  76.6 41.7 %all_to_all.15 = f32[128,21,2,128]{3,2,1,0:T(2,128)S(1)} all-to-all(f32[128,21,2,128]{3,2,1,0:T(2,128)S(1)} %bitcast.16), channel_id=1, replica_groups=mesh['rt'=32,'mob'=4] {'rt','mob'}, dimensions={0} | all-to-all | bytes 5505024 | tf_op jit(solution)/shard_map/all_to_all | solution.py:444
  118.3 1.6 %cross.1 = f32[32,4,8,256]{3,2,1,0:T(8,128)S(1)} custom-call(f32[5376,128]{1,0:T(8,128)S(1)} %bitcast.14), custom_call_target="tpu_custom_call" | custom-call | flops 5000000000 | bytes 15000000 | tf_op jit(solution)/shard_map/cross/pallas_call | solution.py:447
  119.9 0.0 copy-start
  119.9 1.0 copy-done
  120.9 5.6 %all-to-all-start.2 = ((f32[128,8,256]{2,1,0:T(8,128)}), f32[128,8,256]{2,1,0:T(8,128)}, u32[]{:S(2)}, u32[]{:S(2)}) async-start(f32[128,8,256]{2,1,0:T(8,128)} %bitcast.18), calls=%async_computation.2 | async-start | bytes 2097152 | tf_op jit(solution)/shard_map/all_to_all | solution.py:461
  126.5 0.0 copy-done.5
  126.5 0.0 copy-done.6
  126.5 0.1 compare_convert_fusion.mask_ref
  126.6 3.9 %unpack.1 = f32[5120,128]{1,0:T(8,128)} custom-call(f32[5376,128]{1,0:T(8,128)S(1)} %bitcast.15), custom_call_target="tpu_custom_call" | custom-call | flops 5000000000 | bytes 15000000 | tf_op jit(solution)/shard_map/unpack/pallas_call | solution.py:462
  130.4 14.9 %all-to-all-done.2.sums_ref = f32[128,8,256]{2,1,0:T(8,128)} async-done(((f32[128,8,256]{2,1,0:T(8,128)}), f32[128,8,256]{2,1,0:T(8,128)}, u32[]{:S(2)}, u32[]{:S(2)}) %all-to-all-start.2) | async-done | bytes 1048608 | tf_op jit(solution)/shard_map/all_to_all | solution.py:461
  145.4 2.0 %finish.1 = f32[8,256]{1,0:T(8,128)} custom-call(f32[128,8,256]{2,1,0:T(8,128)} %all-to-all-done.2.sums_ref, f32[8,256]{1,0:T(8,128)S(1)} %compare_convert_fusion.mask_ref), custom_call_target="tpu_custom_call" | custom-call | flops 5000000000 | bytes 15000000 | tf_op jit(solution)/shard_map/finish/pallas_call | solution.py:466
  (2 shorter events, 0.0 us)
Async XLA Ops:
  3.9 11.5 %copy-start.1 = (f32[31]{0:T(128)S(1)}, f32[31]{0:T(128)}, u32[]{:S(2)}) copy-start(f32[31]{0:T(128)} %frame_ref.1) | copy-start | bytes 376
  3.9 11.5 %copy-start.2 = (f32[15]{0:T(128)S(1)}, f32[15]{0:T(128)}, u32[]{:S(2)}) copy-start(f32[15]{0:T(128)} %scan_ref.1) | copy-start | bytes 184
  3.9 47.1 %all-to-all-start = ((f32[128,40,128]{2,1,0:T(8,128)}), f32[128,40,128]{2,1,0:T(8,128)S(1)}, u32[]{:S(2)}, u32[]{:S(2)}) async-start(f32[128,40,128]{2,1,0:T(8,128)} %pack.1), calls=%async_computation | async-start | bytes 5242880 | tf_op jit(solution)/shard_map/all_to_all | solution.py:423
  18.0 0.8 copy-start.3
  51.0 1.0 copy-start.4
  118.3 8.2 %copy-start.5 = (s32[256]{0:T(256)S(1)}, s32[256]{0:T(256)}, u32[]{:S(2)}) copy-start(s32[256]{0:T(256)} %param.9) | copy-start | bytes 3076
  118.3 8.2 %copy-start.6 = (s32[8]{0:T(128)S(1)}, s32[8]{0:T(128)}, u32[]{:S(2)}) copy-start(s32[8]{0:T(128)} %param.8) | copy-start | bytes 100
  119.9 1.0 copy-start
  120.9 24.5 %all-to-all-start.2 = ((f32[128,8,256]{2,1,0:T(8,128)}), f32[128,8,256]{2,1,0:T(8,128)}, u32[]{:S(2)}, u32[]{:S(2)}) async-start(f32[128,8,256]{2,1,0:T(8,128)} %bitcast.18), calls=%async_computation.2 | async-start | bytes 2097152 | tf_op jit(solution)/shard_map/all_to_all | solution.py:461

commit v4 on v3

--- a/solution.py
+++ b/solution.py
@@ -140,12 +140,8 @@
     narrow = (lane % (2 * width)) < width
     pairs = []
     for a, b in ((first, third), (second, fourth)):
-        pairs.append(
-            (
-                jnp.where(wide, a, pltpu.roll(b, 2 * width, 1)),
-                jnp.where(wide, pltpu.roll(a, 2 * width, 1), b),
-            )
-        )
+        other = pltpu.roll(jnp.where(wide, b, a), 2 * width, 1)
+        pairs.append((jnp.where(wide, a, other), jnp.where(wide, other, b)))
     out = []
     for a, b in zip(pairs[0], pairs[1]):
         out.append(jnp.where(narrow, a, pltpu.roll(b, width, 1)))
@@ -154,18 +150,8 @@
 
 
 def deblur_kernel(
-    p_ref, wf_hbm, wa_hbm, sf_hbm, sa_hbm, out_ref,
-    wf_ref, wa_ref, sf_ref, sa_ref, obs_ref, est_ref, left_ref, back_ref, mean_ref, band_sem,
-    *, frames, mobs, rows, cells,
+    p_ref, wf_ref, wa_ref, sf_ref, sa_ref, out_ref, obs_ref, est_ref, left_ref, back_ref, mean_ref, *, frames, mobs, rows, cells
 ):
-    copies = [
-        pltpu.make_async_copy(source, target, band_sem.at[i])
-        for i, (source, target) in enumerate(
-            ((sf_hbm, sf_ref), (wf_hbm, wf_ref), (wa_hbm, wa_ref), (sa_hbm, sa_ref))
-        )
-    ]
-    for copy in copies:
-        copy.start()
     owners = LANES
     out_rows = out_ref.shape[0] // owners
     units, blocks, group, width = obs_ref.shape
@@ -289,8 +275,6 @@
     mean_ref[...] = jnp.zeros_like(mean_ref)
     for u in members:
         gather(u, u)
-    for copy in copies:
-        copy.wait()
     for iteration in range(ITERS):
         for u in members:
             forward(u, iteration)
@@ -309,13 +293,12 @@
         out_ref[owner * out_rows + rows : (owner + 1) * out_rows, :] = mean_ref[0:STATS, :]
 
 
-def cross_kernel(q_ref, cross_hbm, centered_ref, cross_ref, out_sem, *, quads):
+def cross_kernel(q_ref, cross_ref, centered_ref, *, quads):
     owners = LANES
     stride = q_ref.shape[0] // owners
     channels = centered_ref.shape[0]
     tiles = channels // LANES
-    column_shards, row_shards, shard_rows, wide = cross_ref.shape
-    copies = []
+    row_shards, column_shards, shard_rows, wide = cross_ref.shape
     stats = q_ref[pl.ds(tiles * quads, owners, stride=stride), :]
     stats_t = stats.T
     for k in range(tiles):
@@ -333,11 +316,7 @@
         )
         first = LANES // 2 + (PREC + m * wide) // LANES
         column = jnp.concatenate([stats_t[first + i : first + i + 1] for i in range(wide // LANES)], axis=1)
-        cross_ref[m] = (cross * row * column).reshape(row_shards, shard_rows, wide)
-        copies.append(pltpu.make_async_copy(cross_ref.at[m], cross_hbm.at[:, m], out_sem.at[m]))
-        copies[-1].start()
-    for copy in copies:
-        copy.wait()
+        cross_ref[:, m] = (cross * row * column).reshape(row_shards, shard_rows, wide)
 
 
 def finish_kernel(sums_ref, mask_ref, out_ref):
@@ -425,17 +404,15 @@
         deblur_kernel,
         "deblur",
         shape((owners * out_rows, LANES), F32),
-        [vmem] + [hbm] * 4,
-        [pltpu.VMEM(band.shape, BF16) for band in bands]
-        + [
+        [vmem] * 5,
+        [
             pltpu.VMEM((rows // 8, blocks, group, BLOCK), F32),
             pltpu.VMEM((rows // 8, blocks, group, BLOCK), F32),
             pltpu.VMEM((rows // 8, blocks * group, 2 * BLOCK + 2 * HALO), BF16),
             pltpu.VMEM((rows // 8, blocks * group, 2 * BLOCK + 2 * HALO), BF16),
             pltpu.VMEM((8, LANES), F32),
-            pltpu.SemaphoreType.DMA((len(bands),)),
         ],
-        mib=40,
+        mib=24,
         frames=frames,
         mobs=mobs,
         rows=rows,
@@ -449,13 +426,7 @@
         "cross",
         shape((row_shards, mobs, PREC // row_shards, width), F32),
         [vmem],
-        [
-            pltpu.VMEM((channels, cells), BF16),
-            pltpu.VMEM((mobs, row_shards, PREC // row_shards, width), F32),
-            pltpu.SemaphoreType.DMA((mobs,)),
-        ],
-        out_spec=hbm,
-        mib=16,
+        [pltpu.VMEM((channels, cells), BF16)],
         quads=quads,
     )(returned)
     sums = lax.all_to_all(cross.reshape(owners, PREC // row_shards, width), AXES, 0, 0, tiled=True)

time: 148 us -> 136 us (0.919)
  Pallas kernels: 37.7 us -> 26.2 us
    pallas_call x1, Pallas kernels: 24.5 us -> 13.9 us  [local(): call(deblur_kernel, 'deblur', shape((owners * out_rows, LANES), F32), [vm...]
  transfers between devices with their start and end apart: 2 -> 2, of which waited for: 2 -> 2; matrix products, arithmetic and copies ran while one was open for 0% -> 0% of each run, Pallas kernels for 4% -> 5%
where the time goes in v4:
time: 136 us
  waiting for transfers between devices  47.2 us (35%)
  blocking collectives  41.7 us (31%)
  Pallas kernels  26.2 us (19%)
  starting transfers between devices  17.1 us (13%)
  local copies, waits for them, and re-layouts  2.84 us (2%)
    all_to_all x1, blocking collectives, local(): lax.all_to_all(deblurred.reshape(owners, out_rows // STATS, STATS, LANES)...  41.7 us
    all_to_all x1, waiting for transfers between devices, local(): arrived = lax.all_to_all(packed, AXES, 0, 0, tiled=True)  32.2 us
    all_to_all x1, waiting for transfers between devices, local(): lax.all_to_all(cross.reshape(owners, PREC // row_shards, width), AXES, 0,...  14.9 us
    pallas_call x1, Pallas kernels, local(): call(deblur_kernel, 'deblur', shape((owners * out_rows, LANES), F32), [vm...  13.9 us
    all_to_all x1, starting transfers between devices, local(): arrived = lax.all_to_all(packed, AXES, 0, 0, tiled=True)  11.5 us
    all_to_all x1, starting transfers between devices, local(): lax.all_to_all(cross.reshape(owners, PREC // row_shards, width), AXES, 0,...  5.61 us
    pallas_call x1, Pallas kernels, local(): call(unpack_kernel, 'unpack', shape((cells * channels // LANES, LANES), F...  3.85 us
    pallas_call x1, Pallas kernels, local(): call(pack_kernel, 'pack', shape((owners, rows, LANES), F32), [hbm], [pltp...  3.27 us
  transfers between devices with their start and end apart: 2, of which 2 were waited for; matrix products, arithmetic and copies ran while one was open for 0% of the time, Pallas kernels for 5%

profile of v4, /device:TPU:1, one launch (start us, length us, event | category | flops | bytes accessed | tf_op | source)
XLA Modules:
  0.0 135.8 jit_solution(61313003071074996)
XLA Ops:
  0.6 3.3 %pack.1 = f32[128,40,128]{2,1,0:T(8,128)} custom-call(f32[64,10,8,128]{3,2,1,0:T(8,128)} %bitcast.19), custom_call_target="tpu_custom_call" | custom-call | flops 5000000000 | bytes 15000000 | tf_op jit(solution)/shard_map/pack/pallas_call | solution.py:377
  3.9 0.0 copy-start.1
  3.9 0.0 copy-start.2
  3.9 11.5 %all-to-all-start = ((f32[128,40,128]{2,1,0:T(8,128)}), f32[128,40,128]{2,1,0:T(8,128)S(1)}, u32[]{:S(2)}, u32[]{:S(2)}) async-start(f32[128,40,128]{2,1,0:T(8,128)} %pack.1), calls=%async_computation | async-start | bytes 5242880 | tf_op jit(solution)/shard_map/all_to_all | solution.py:402
  15.4 0.0 copy-done.1
  15.4 0.0 copy-done.2
  15.4 2.5 %bands.1 = (bf16[1024,256]{1,0:T(8,128)(2,1)S(1)}, bf16[1024,256]{1,0:T(8,128)(2,1)S(1)}, bf16[256,256]{1,0:T(8,128)(2,1)S(1)}, bf16[256,256]{1,0:T(8,128)(2,1)S(1)}) custom-call(f32[31]{0:T(128)S(1)} %copy-done.1, f32[15]{0:T(128)S(1)} %copy-done.2), custom_call_target="tpu_custom_call" | custom-call | flops 5000000000 | bytes 15000000 | tf_op jit(solution)/shard_map/bands/pallas_call | solution.py:393
  18.0 0.0 copy-start.3
  18.0 0.8 copy-done.3
  18.8 32.2 %all-to-all-done = f32[128,40,128]{2,1,0:T(8,128)S(1)} async-done(((f32[128,40,128]{2,1,0:T(8,128)}), f32[128,40,128]{2,1,0:T(8,128)S(1)}, u32[]{:S(2)}, u32[]{:S(2)}) %all-to-all-start) | async-done | bytes 2621472 | tf_op jit(solution)/shard_map/all_to_all | solution.py:402
  51.0 0.0 copy-start.4
  51.0 1.0 copy-done.4
  52.1 13.9 %deblur.1 = f32[5376,128]{1,0:T(8,128)S(1)} custom-call(f32[5120,128]{1,0:T(8,128)S(1)} %bitcast.17, bf16[1024,256]{1,0:T(8,128)(2,1)S(1)} %get-tuple-element.6.wf_ref, bf16[1024,256]{1,0:T(8,128)(2,1)S(1)} %copy-done.4, bf16[256,256]{1,0:T(8,128)(2,1)S(1)} %get-tuple-element.8.sf_ref, bf16[256,256]{1,0:T(8,128)(2,1)S(1)} %get-tuple-element.9.sa_ref), custom_call_target="tpu_custom_call" | custom-call | flops 5000000000 | bytes 15000000 | tf_op jit(solution)/shard_map/deblur/pallas_call | solution.py:403
  66.0 41.7 %all_to_all.15 = f32[128,21,2,128]{3,2,1,0:T(2,128)S(1)} all-to-all(f32[128,21,2,128]{3,2,1,0:T(2,128)S(1)} %bitcast.16), channel_id=1, replica_groups=mesh['rt'=32,'mob'=4] {'rt','mob'}, dimensions={0} | all-to-all | bytes 5505024 | tf_op jit(solution)/shard_map/all_to_all | solution.py:421
  107.7 0.7 cross.1
  108.3 0.0 copy-start
  108.3 1.0 copy-done
  109.3 5.6 %all-to-all-start.2 = ((f32[128,8,256]{2,1,0:T(8,128)}), f32[128,8,256]{2,1,0:T(8,128)}, u32[]{:S(2)}, u32[]{:S(2)}) async-start(f32[128,8,256]{2,1,0:T(8,128)} %bitcast.18), calls=%async_computation.2 | async-start | bytes 2097152 | tf_op jit(solution)/shard_map/all_to_all | solution.py:432
  114.9 0.0 copy-done.5
  114.9 0.0 copy-done.6
  115.0 0.1 compare_convert_fusion.mask_ref
  115.0 3.9 %unpack.1 = f32[5120,128]{1,0:T(8,128)} custom-call(f32[5376,128]{1,0:T(8,128)S(1)} %bitcast.15), custom_call_target="tpu_custom_call" | custom-call | flops 5000000000 | bytes 15000000 | tf_op jit(solution)/shard_map/unpack/pallas_call | solution.py:433
  118.9 14.9 %all-to-all-done.2.sums_ref = f32[128,8,256]{2,1,0:T(8,128)} async-done(((f32[128,8,256]{2,1,0:T(8,128)}), f32[128,8,256]{2,1,0:T(8,128)}, u32[]{:S(2)}, u32[]{:S(2)}) %all-to-all-start.2) | async-done | bytes 1048608 | tf_op jit(solution)/shard_map/all_to_all | solution.py:432
  133.8 2.0 %finish.1 = f32[8,256]{1,0:T(8,128)} custom-call(f32[128,8,256]{2,1,0:T(8,128)} %all-to-all-done.2.sums_ref, f32[8,256]{1,0:T(8,128)S(1)} %compare_convert_fusion.mask_ref), custom_call_target="tpu_custom_call" | custom-call | flops 5000000000 | bytes 15000000 | tf_op jit(solution)/shard_map/finish/pallas_call | solution.py:437
  (2 shorter events, 0.0 us)
Async XLA Ops:
  3.9 11.5 %copy-start.1 = (f32[31]{0:T(128)S(1)}, f32[31]{0:T(128)}, u32[]{:S(2)}) copy-start(f32[31]{0:T(128)} %frame_ref.1) | copy-start | bytes 376
  3.9 11.5 %copy-start.2 = (f32[15]{0:T(128)S(1)}, f32[15]{0:T(128)}, u32[]{:S(2)}) copy-start(f32[15]{0:T(128)} %scan_ref.1) | copy-start | bytes 184
  3.9 47.1 %all-to-all-start = ((f32[128,40,128]{2,1,0:T(8,128)}), f32[128,40,128]{2,1,0:T(8,128)S(1)}, u32[]{:S(2)}, u32[]{:S(2)}) async-start(f32[128,40,128]{2,1,0:T(8,128)} %pack.1), calls=%async_computation | async-start | bytes 5242880 | tf_op jit(solution)/shard_map/all_to_all | solution.py:402
  18.0 0.8 copy-start.3
  51.0 1.0 copy-start.4
  107.7 7.3 %copy-start.5 = (s32[256]{0:T(256)S(1)}, s32[256]{0:T(256)}, u32[]{:S(2)}) copy-start(s32[256]{0:T(256)} %param.9) | copy-start | bytes 3076
  107.7 7.3 %copy-start.6 = (s32[8]{0:T(128)S(1)}, s32[8]{0:T(128)}, u32[]{:S(2)}) copy-start(s32[8]{0:T(128)} %param.8) | copy-start | bytes 100
  108.3 1.0 copy-start
  109.3 24.5 %all-to-all-start.2 = ((f32[128,8,256]{2,1,0:T(8,128)}), f32[128,8,256]{2,1,0:T(8,128)}, u32[]{:S(2)}, u32[]{:S(2)}) async-start(f32[128,8,256]{2,1,0:T(8,128)} %bitcast.18), calls=%async_computation.2 | async-start | bytes 2097152 | tf_op jit(solution)/shard_map/all_to_all | solution.py:432

commit v5 on v4

--- a/solution.py
+++ b/solution.py
@@ -12,9 +12,9 @@
 LANES = 128
 AXES = ("rt", "mob")
 BLOCK = 256
+CORES = 2
 EDGE = 16
-TOGETHER = 2
-STATS = 2
+STATS = 1
 HALO = 128
 
 F32 = jnp.float32
@@ -167,8 +167,11 @@
 
     def scan_blur(values, matrix):
         high, low = split(values)
-        both = jnp.dot(matrix, jnp.concatenate([high, low], axis=0), preferred_element_type=F32)
-        return both[0:group] + both[group : 2 * group]
+        return scan_product(matrix, jnp.concatenate([high, low], axis=0))
+
+    def scan_product(matrix, both):
+        out = jnp.dot(matrix, both, preferred_element_type=F32)
+        return out[0:group] + out[group : 2 * group]
 
     def put(ref, u, n, values):
         high, low = split(values)
@@ -192,16 +195,15 @@
                     halo = jnp.where(again, pltpu.roll(halo, 2 * EDGE, 1), halo)
                 ref[u, here, 2 * width + which * HALO : 2 * width + (which + 1) * HALO] = halo
 
-    def frame_blur(ref, members, matrix):
+    def frame_blur(ref, chunks, matrix):
         lhs = []
-        for u in members:
-            center, rest = ref[u, :, 0 : 2 * width], ref[u, :, 2 * width : 2 * width + 2 * HALO]
+        for u, first, count in chunks:
+            here = slice(first * group, (first + count) * group)
+            center, rest = ref[u, here, 0 : 2 * width], ref[u, here, 2 * width : 2 * width + 2 * HALO]
             lhs.append(jnp.concatenate([center, center[:, 0:width], rest], axis=1))
         out = jnp.dot(jnp.concatenate(lhs, axis=0), matrix, preferred_element_type=F32)
-        return {
-            u: [out[(k * blocks + n) * group : (k * blocks + n + 1) * group] for n in range(blocks)]
-            for k, u in enumerate(members)
-        }
+        places = [(u, first + n) for u, first, count in chunks for n in range(count)]
+        return [(u, n, out[i * group : (i + 1) * group]) for i, (u, n) in enumerate(places)]
 
     def total8(parts):
         acc = None
@@ -241,15 +243,20 @@
             put(left_ref, u, n, scan_blur(estimate[u, n], sf_ref[...]))
         put_halo(left_ref, u)
 
-    def ratios(u, done):
-        for n, blurred in enumerate(done[u]):
+    def ratios(chunks):
+        for u, n, blurred in frame_blur(left_ref, chunks, wf_ref[...]):
             put(back_ref, u, n, obs_ref[u, n] / blurred)
-        put_halo(back_ref, u)
-
-    def adjoint(u, iteration, done):
+
+    def adjoint_frames(chunks):
+        for u, n, blurred in frame_blur(back_ref, chunks, wa_ref[...]):
+            put(left_ref, u, n, blurred)
+
+    def adjoint_scans(u, iteration):
         estimate = obs_ref if iteration == 0 else est_ref
-        for n, blurred in enumerate(done[u]):
-            est_ref[u, n] = estimate[u, n] * scan_blur(blurred, sa_ref[...])
+        for n in range(blocks):
+            here = slice(n * group, (n + 1) * group)
+            both = jnp.concatenate([left_ref[u, here, 0:width], left_ref[u, here, width : 2 * width]], axis=0)
+            est_ref[u, n] = estimate[u, n] * scan_product(sa_ref[...], both)
 
     def statistics(u, pair):
         upper, lower = total8([est_ref[u, n] for n in range(blocks)])
@@ -271,21 +278,21 @@
         mean_ref[...] = held
 
     members = range(units)
-    sets = [members[first : first + TOGETHER] for first in range(0, units, TOGETHER)]
+    sets = [[(u, 0, blocks)] for u in members]
     mean_ref[...] = jnp.zeros_like(mean_ref)
     for u in members:
         gather(u, u)
     for iteration in range(ITERS):
         for u in members:
             forward(u, iteration)
-        for some in sets:
-            done = frame_blur(left_ref, some, wf_ref[...])
-            for u in some:
-                ratios(u, done)
-        for some in sets:
-            done = frame_blur(back_ref, some, wa_ref[...])
-            for u in some:
-                adjoint(u, iteration, done)
+        for chunks in sets:
+            ratios(chunks)
+        for u in members:
+            put_halo(back_ref, u)
+        for chunks in sets:
+            adjoint_frames(chunks)
+        for u in members:
+            adjoint_scans(u, iteration)
     for u in members:
         statistics(u, u)
         scatter(u, u)
@@ -293,12 +300,13 @@
         out_ref[owner * out_rows + rows : (owner + 1) * out_rows, :] = mean_ref[0:STATS, :]
 
 
-def cross_kernel(q_ref, cross_ref, centered_ref, *, quads):
+def cross_kernel(q_ref, keep_ref, send_ref, centered_ref, *, quads):
     owners = LANES
     stride = q_ref.shape[0] // owners
+    core = lax.axis_index("mob") % CORES
     channels = centered_ref.shape[0]
     tiles = channels // LANES
-    row_shards, column_shards, shard_rows, wide = cross_ref.shape
+    row_shards, chips, shard_rows, wide = keep_ref.shape
     stats = q_ref[pl.ds(tiles * quads, owners, stride=stride), :]
     stats_t = stats.T
     for k in range(tiles):
@@ -307,7 +315,7 @@
             block = q_ref[pl.ds(k * quads + q, owners, stride=stride), :]
             centered_ref[k * LANES : (k + 1) * LANES, q * LANES : (q + 1) * LANES] = (block - mean).astype(BF16)
     row = jnp.concatenate([stats[:, LANES // 2 + k : LANES // 2 + k + 1] for k in range(PREC // LANES)], axis=0)
-    for m in range(column_shards):
+    for m in range(chips * CORES):
         cross = lax.dot_general(
             centered_ref[:PREC, :],
             centered_ref[PREC + m * wide : PREC + (m + 1) * wide, :],
@@ -316,7 +324,13 @@
         )
         first = LANES // 2 + (PREC + m * wide) // LANES
         column = jnp.concatenate([stats_t[first + i : first + i + 1] for i in range(wide // LANES)], axis=1)
-        cross_ref[:, m] = (cross * row * column).reshape(row_shards, shard_rows, wide)
+        cross = (cross * row * column).reshape(row_shards, shard_rows, wide)
+
+        def store(ref, cross=cross, chip=m // CORES):
+            ref[:, chip] = cross
+
+        pl.when(core == m % CORES)(functools.partial(store, keep_ref))
+        pl.when(core != m % CORES)(functools.partial(store, send_ref))
 
 
 def finish_kernel(sums_ref, mask_ref, out_ref):
@@ -421,15 +435,15 @@
     returned = lax.all_to_all(
         deblurred.reshape(owners, out_rows // STATS, STATS, LANES), AXES, 0, 0, tiled=True
     ).reshape(owners * out_rows, LANES)
-    cross = call(
-        cross_kernel,
-        "cross",
-        shape((row_shards, mobs, PREC // row_shards, width), F32),
-        [vmem],
-        [pltpu.VMEM((channels, cells), BF16)],
-        quads=quads,
+    half = shape((row_shards, mobs // CORES, PREC // row_shards, width), F32)
+    keep, send = call(
+        cross_kernel, "cross", (half, half), [vmem], [pltpu.VMEM((channels, cells), BF16)], quads=quads
     )(returned)
-    sums = lax.all_to_all(cross.reshape(owners, PREC // row_shards, width), AXES, 0, 0, tiled=True)
+    both = keep + lax.ppermute(send, "mob", [(m, m ^ 1) for m in range(mobs)])
+    groups = [[first + CORES * d for d in range(owners // CORES)] for first in range(CORES)]
+    sums = lax.all_to_all(
+        both.reshape(owners // CORES, PREC // row_shards, width), AXES, 0, 0, axis_index_groups=groups, tiled=True
+    )
     estimate = call(
         unpack_kernel, "unpack", shape((cells * channels // LANES, LANES), F32), [vmem], frames=frames, scans=scans
     )(returned)

time: 136 us -> 129 us (0.949)
  waiting for transfers between devices: 47.2 us -> 42.4 us
  Pallas kernels: 26.2 us -> 23.6 us
    all_to_all x1, waiting for transfers between devices: 14.9 us -> 8.36 us  [local(): lax.all_to_all(both.reshape(owners // CORES, PREC // row_shards, width),...]
    pallas_call x1, Pallas kernels: 13.9 us -> 11.8 us  [local(): call(deblur_kernel, 'deblur', shape((owners * out_rows, LANES), F32), [vm...]
    ppermute x0 -> x1, waiting for transfers between devices: none -> 1.82 us  [local(): both = keep + lax.ppermute(send, 'mob', [(m, m ^ 1) for m in range(mobs)])]
    unnamed x14 -> x12, local copies, waits for them, and re-layouts: 2.84 us -> 1.86 us
  transfers between devices with their start and end apart: 2 -> 3, of which waited for: 2 -> 3; matrix products, arithmetic and copies ran while one was open for 0% -> 0% of each run, Pallas kernels for 5% -> 5%
where the time goes in v5:
time: 129 us; the launch traced here: 128 us
  waiting for transfers between devices  42.4 us (33%)
  blocking collectives  41 us (32%)
  Pallas kernels  23.6 us (18%)
  starting transfers between devices  17.5 us (14%)
  local copies, waits for them, and re-layouts  1.86 us (1%)
    all_to_all x1, blocking collectives, local(): lax.all_to_all(deblurred.reshape(owners, out_rows // STATS, STATS, LANES)...  41 us
    all_to_all x1, waiting for transfers between devices, local(): arrived = lax.all_to_all(packed, AXES, 0, 0, tiled=True)  32.2 us
    pallas_call x1, Pallas kernels, local(): call(deblur_kernel, 'deblur', shape((owners * out_rows, LANES), F32), [vm...  11.8 us
    all_to_all x1, starting transfers between devices, local(): arrived = lax.all_to_all(packed, AXES, 0, 0, tiled=True)  11.5 us
    all_to_all x1, waiting for transfers between devices, local(): lax.all_to_all(both.reshape(owners // CORES, PREC // row_shards, width),...  8.36 us
    all_to_all x1, starting transfers between devices, local(): lax.all_to_all(both.reshape(owners // CORES, PREC // row_shards, width),...  5.8 us
    pallas_call x1, Pallas kernels, local(): call(unpack_kernel, 'unpack', shape((cells * channels // LANES, LANES), F...  3.85 us
    pallas_call x1, Pallas kernels, local(): call(pack_kernel, 'pack', shape((owners, rows, LANES), F32), [hbm], [pltp...  3.27 us
  transfers between devices with their start and end apart: 3, of which 3 were waited for; matrix products, arithmetic and copies ran while one was open for 0% of the time, Pallas kernels for 5%

profile of v5, /device:TPU:1, one launch (start us, length us, event | category | flops | bytes accessed | tf_op | source)
XLA Modules:
  0.0 128.1 jit_solution(6840409153797291659)
XLA Ops:
  0.6 3.3 %pack.1 = f32[128,40,128]{2,1,0:T(8,128)} custom-call(f32[64,10,8,128]{3,2,1,0:T(8,128)} %bitcast.19), custom_call_target="tpu_custom_call" | custom-call | flops 5000000000 | bytes 15000000 | tf_op jit(solution)/shard_map/pack/pallas_call | solution.py:391
  3.9 0.0 copy-start
  3.9 0.0 copy-start.1
  3.9 11.5 %all-to-all-start = ((f32[128,40,128]{2,1,0:T(8,128)}), f32[128,40,128]{2,1,0:T(8,128)S(1)}, u32[]{:S(2)}, u32[]{:S(2)}) async-start(f32[128,40,128]{2,1,0:T(8,128)} %pack.1), calls=%async_computation | async-start | bytes 5242880 | tf_op jit(solution)/shard_map/all_to_all | solution.py:416
  15.4 0.0 copy-done
  15.4 0.0 copy-done.1
  15.4 2.5 %bands.1 = (bf16[1024,256]{1,0:T(8,128)(2,1)S(1)}, bf16[1024,256]{1,0:T(8,128)(2,1)S(1)}, bf16[256,256]{1,0:T(8,128)(2,1)S(1)}, bf16[256,256]{1,0:T(8,128)(2,1)S(1)}) custom-call(f32[31]{0:T(128)S(1)} %copy-done, f32[15]{0:T(128)S(1)} %copy-done.1), custom_call_target="tpu_custom_call" | custom-call | flops 5000000000 | bytes 15000000 | tf_op jit(solution)/shard_map/bands/pallas_call | solution.py:407
  18.0 0.0 copy-start.2
  18.0 0.8 copy-done.2
  18.8 32.2 %all-to-all-done = f32[128,40,128]{2,1,0:T(8,128)S(1)} async-done(((f32[128,40,128]{2,1,0:T(8,128)}), f32[128,40,128]{2,1,0:T(8,128)S(1)}, u32[]{:S(2)}, u32[]{:S(2)}) %all-to-all-start) | async-done | bytes 2621472 | tf_op jit(solution)/shard_map/all_to_all | solution.py:416
  51.0 1.0 copy-done.3
  52.1 11.8 %deblur.1 = f32[5248,128]{1,0:T(8,128)S(1)} custom-call(f32[5120,128]{1,0:T(8,128)S(1)} %bitcast.17, bf16[1024,256]{1,0:T(8,128)(2,1)S(1)} %get-tuple-element.8.wf_ref, bf16[1024,256]{1,0:T(8,128)(2,1)S(1)} %copy-done.3, bf16[256,256]{1,0:T(8,128)(2,1)S(1)} %get-tuple-element.10.sf_ref, bf16[256,256]{1,0:T(8,128)(2,1)S(1)} %get-tuple-element.11.sa_ref), custom_call_target="tpu_custom_call" | custom-call | flops 5000000000 | bytes 15000000 | tf_op jit(solution)/shard_map/deblur/pallas_call | solution.py:417
  63.8 41.0 %all_to_all.15 = f32[128,41,1,128]{3,2,1,0:T(1,128)S(1)} all-to-all(f32[128,41,1,128]{3,2,1,0:T(1,128)S(1)} %bitcast.16), channel_id=1, replica_groups=mesh['rt'=32,'mob'=4] {'rt','mob'}, dimensions={0} | all-to-all | bytes 5373952 | tf_op jit(solution)/shard_map/all_to_all | solution.py:435
  104.9 1.5 %cross.1 = (f32[32,2,8,256]{3,2,1,0:T(8,128)S(1)}, f32[32,2,8,256]{3,2,1,0:T(8,128)S(1)}) custom-call(f32[5248,128]{1,0:T(8,128)S(1)} %bitcast.14), custom_call_target="tpu_custom_call" | custom-call | flops 5000000000 | bytes 15000000 | tf_op jit(solution)/shard_map/cross/pallas_call | solution.py:439
  106.4 0.0 copy-start.4
  106.4 0.0 copy-start.5
  106.4 0.2 collective-permute-start
  106.6 1.8 %collective-permute-done = f32[32,2,8,256]{3,2,1,0:T(8,128)S(1)} collective-permute-done((f32[32,2,8,256]{3,2,1,0:T(8,128)S(1)}, f32[32,2,8,256]{3,2,1,0:T(8,128)S(1)}, u32[]{:S(2)}, u32[]{:S(2)}) %collective-permute-start) | collective-permute-done | bytes 524320 | tf_op jit(solution)/shard_map/ppermute | solution.py:442
  108.4 0.9 add.3
  109.3 5.8 %all-to-all-start.2 = ((f32[64,8,256]{2,1,0:T(8,128)}), f32[64,8,256]{2,1,0:T(8,128)S(1)}, u32[]{:S(2)}, u32[]{:S(2)}) async-start(f32[64,8,256]{2,1,0:T(8,128)} %bitcast.18), calls=%async_computation.2 | async-start | bytes 1048576 | tf_op jit(solution)/shard_map/all_to_all | solution.py:444
  115.1 0.1 compare_convert_fusion.mask_ref
  115.2 3.9 %unpack.1 = f32[5120,128]{1,0:T(8,128)} custom-call(f32[5248,128]{1,0:T(8,128)S(1)} %bitcast.15), custom_call_target="tpu_custom_call" | custom-call | flops 5000000000 | bytes 15000000 | tf_op jit(solution)/shard_map/unpack/pallas_call | solution.py:447
  119.0 8.4 %all-to-all-done.2.sums_ref = f32[64,8,256]{2,1,0:T(8,128)S(1)} async-done(((f32[64,8,256]{2,1,0:T(8,128)}), f32[64,8,256]{2,1,0:T(8,128)S(1)}, u32[]{:S(2)}, u32[]{:S(2)}) %all-to-all-start.2) | async-done | bytes 524320 | tf_op jit(solution)/shard_map/all_to_all | solution.py:444
  127.4 0.7 finish.1
  (3 shorter events, 0.0 us)
Async XLA Ops:
  3.9 11.5 %copy-start = (f32[31]{0:T(128)S(1)}, f32[31]{0:T(128)}, u32[]{:S(2)}) copy-start(f32[31]{0:T(128)} %frame_ref.1) | copy-start | bytes 376
  3.9 11.5 %copy-start.1 = (f32[15]{0:T(128)S(1)}, f32[15]{0:T(128)}, u32[]{:S(2)}) copy-start(f32[15]{0:T(128)} %scan_ref.1) | copy-start | bytes 184
  3.9 47.1 %all-to-all-start = ((f32[128,40,128]{2,1,0:T(8,128)}), f32[128,40,128]{2,1,0:T(8,128)S(1)}, u32[]{:S(2)}, u32[]{:S(2)}) async-start(f32[128,40,128]{2,1,0:T(8,128)} %pack.1), calls=%async_computation | async-start | bytes 5242880 | tf_op jit(solution)/shard_map/all_to_all | solution.py:416
  18.0 0.8 copy-start.2
  51.0 1.0 copy-start.3
  106.4 8.7 %copy-start.4 = (s32[256]{0:T(256)S(1)}, s32[256]{0:T(256)}, u32[]{:S(2)}) copy-start(s32[256]{0:T(256)} %param.9) | copy-start | bytes 3076
  106.4 8.7 %copy-start.5 = (s32[8]{0:T(128)S(1)}, s32[8]{0:T(128)}, u32[]{:S(2)}) copy-start(s32[8]{0:T(128)} %param.8) | copy-start | bytes 100
  106.4 2.0 %collective-permute-start = (f32[32,2,8,256]{3,2,1,0:T(8,128)S(1)}, f32[32,2,8,256]{3,2,1,0:T(8,128)S(1)}, u32[]{:S(2)}, u32[]{:S(2)}) collective-permute-start(f32[32,2,8,256]{3,2,1,0:T(8,128)S(1)} %get-tuple-element.13), channel_id=1, source_target_pairs={{0,1},{1,0},{2,3},{3,2},{4,5},{5,4},{6,7},{7,6},{8,9},{9,8},{10,11... | collective-permute-start | bytes 1572872 | tf_op jit(solution)/shard_map/ppermute | solution.py:442
  109.3 18.1 %all-to-all-start.2 = ((f32[64,8,256]{2,1,0:T(8,128)}), f32[64,8,256]{2,1,0:T(8,128)S(1)}, u32[]{:S(2)}, u32[]{:S(2)}) async-start(f32[64,8,256]{2,1,0:T(8,128)} %bitcast.18), calls=%async_computation.2 | async-start | bytes 1048576 | tf_op jit(solution)/shard_map/all_to_all | solution.py:444

commit v6 on v5

--- a/solution.py
+++ b/solution.py
@@ -87,7 +87,7 @@
         leave(step).wait()
 
 
-def bands_kernel(frame_ref, scan_ref, wf_ref, wa_ref, sf_ref, sa_ref, *, scans, per_lane):
+def bands_kernel(frame_ref, scan_ref, sf_ref, sa_ref, wf_ref, wa_ref, *, scans, per_lane):
     frame_radius, scan_radius = (frame_ref.shape[0] - 1) // 2, (scan_ref.shape[0] - 1) // 2
     quads = scans // per_lane
     group = sf_ref.shape[0] // 2
@@ -150,7 +150,7 @@
 
 
 def deblur_kernel(
-    p_ref, wf_ref, wa_ref, sf_ref, sa_ref, out_ref, obs_ref, est_ref, left_ref, back_ref, mean_ref, *, frames, mobs, rows, cells
+    p_ref, sf_ref, sa_ref, wf_ref, wa_ref, out_ref, obs_ref, est_ref, left_ref, back_ref, mean_ref, *, frames, mobs, rows, cells
 ):
     owners = LANES
     out_rows = out_ref.shape[0] // owners
@@ -315,7 +315,8 @@
             block = q_ref[pl.ds(k * quads + q, owners, stride=stride), :]
             centered_ref[k * LANES : (k + 1) * LANES, q * LANES : (q + 1) * LANES] = (block - mean).astype(BF16)
     row = jnp.concatenate([stats[:, LANES // 2 + k : LANES // 2 + k + 1] for k in range(PREC // LANES)], axis=0)
-    for m in range(chips * CORES):
+
+    def product(m):
         cross = lax.dot_general(
             centered_ref[:PREC, :],
             centered_ref[PREC + m * wide : PREC + (m + 1) * wide, :],
@@ -324,13 +325,12 @@
         )
         first = LANES // 2 + (PREC + m * wide) // LANES
         column = jnp.concatenate([stats_t[first + i : first + i + 1] for i in range(wide // LANES)], axis=1)
-        cross = (cross * row * column).reshape(row_shards, shard_rows, wide)
-
-        def store(ref, cross=cross, chip=m // CORES):
-            ref[:, chip] = cross
-
-        pl.when(core == m % CORES)(functools.partial(store, keep_ref))
-        pl.when(core != m % CORES)(functools.partial(store, send_ref))
+        return (cross * row * column).reshape(row_shards, shard_rows, wide)
+
+    for chip in range(chips):
+        even, odd = product(chip * CORES), product(chip * CORES + 1)
+        keep_ref[:, chip] = jnp.where(core == 0, even, odd)
+        send_ref[:, chip] = jnp.where(core == 0, odd, even)
 
 
 def finish_kernel(sums_ref, mask_ref, out_ref):
@@ -407,7 +407,7 @@
     bands = call(
         bands_kernel,
         "bands",
-        (shape((depth, BLOCK), BF16),) * 2 + (shape((2 * group, 2 * group), BF16),) * 2,
+        (shape((2 * group, 2 * group), BF16),) * 2 + (shape((depth, BLOCK), BF16),) * 2,
         [smem, smem],
         mib=16,
         scans=scans,
@@ -426,7 +426,7 @@
             pltpu.VMEM((rows // 8, blocks * group, 2 * BLOCK + 2 * HALO), BF16),
             pltpu.VMEM((8, LANES), F32),
         ],
-        mib=24,
+        mib=18,
         frames=frames,
         mobs=mobs,
         rows=rows,

time: 129 us -> 128 us (level)
  no operation moved by 1% of the time
where the time goes in v6:
time: 128 us; the launch traced here: 127 us
  waiting for transfers between devices  42.4 us (33%)
  blocking collectives  41 us (32%)
  Pallas kernels  22.8 us (18%)
  starting transfers between devices  17.5 us (14%)
  local copies, waits for them, and re-layouts  1.86 us (1%)
    all_to_all x1, blocking collectives, local(): lax.all_to_all(deblurred.reshape(owners, out_rows // STATS, STATS, LANES)...  41 us
    all_to_all x1, waiting for transfers between devices, local(): arrived = lax.all_to_all(packed, AXES, 0, 0, tiled=True)  32.2 us
    pallas_call x1, Pallas kernels, local(): call(deblur_kernel, 'deblur', shape((owners * out_rows, LANES), F32), [vm...  11.8 us
    all_to_all x1, starting transfers between devices, local(): arrived = lax.all_to_all(packed, AXES, 0, 0, tiled=True)  11.5 us
    all_to_all x1, waiting for transfers between devices, local(): lax.all_to_all(both.reshape(owners // CORES, PREC // row_shards, width),...  8.36 us
    all_to_all x1, starting transfers between devices, local(): lax.all_to_all(both.reshape(owners // CORES, PREC // row_shards, width),...  5.81 us
    pallas_call x1, Pallas kernels, local(): call(unpack_kernel, 'unpack', shape((cells * channels // LANES, LANES), F...  3.85 us
    pallas_call x1, Pallas kernels, local(): call(pack_kernel, 'pack', shape((owners, rows, LANES), F32), [hbm], [pltp...  3.27 us
  transfers between devices with their start and end apart: 3, of which 3 were waited for; matrix products, arithmetic and copies ran while one was open for 0% of the time, Pallas kernels for 5%

profile of v6, /device:TPU:1, one launch (start us, length us, event | category | flops | bytes accessed | tf_op | source)
XLA Modules:
  0.0 127.2 jit_solution(937600706950403832)
XLA Ops:
  0.6 3.3 %pack.1 = f32[128,40,128]{2,1,0:T(8,128)} custom-call(f32[64,10,8,128]{3,2,1,0:T(8,128)} %bitcast.19), custom_call_target="tpu_custom_call" | custom-call | flops 5000000000 | bytes 15000000 | tf_op jit(solution)/shard_map/pack/pallas_call | solution.py:391
  3.9 0.0 copy-start
  3.9 0.0 copy-start.1
  3.9 11.5 %all-to-all-start = ((f32[128,40,128]{2,1,0:T(8,128)}), f32[128,40,128]{2,1,0:T(8,128)S(1)}, u32[]{:S(2)}, u32[]{:S(2)}) async-start(f32[128,40,128]{2,1,0:T(8,128)} %pack.1), calls=%async_computation | async-start | bytes 5242880 | tf_op jit(solution)/shard_map/all_to_all | solution.py:416
  15.4 0.0 copy-done
  15.4 0.0 copy-done.1
  15.4 2.5 %bands.1 = (bf16[256,256]{1,0:T(8,128)(2,1)S(1)}, bf16[256,256]{1,0:T(8,128)(2,1)S(1)}, bf16[1024,256]{1,0:T(8,128)(2,1)S(1)}, bf16[1024,256]{1,0:T(8,128)(2,1)S(1)}) custom-call(f32[31]{0:T(128)S(1)} %copy-done, f32[15]{0:T(128)S(1)} %copy-done.1), custom_call_target="tpu_custom_call" | custom-call | flops 5000000000 | bytes 15000000 | tf_op jit(solution)/shard_map/bands/pallas_call | solution.py:407
  18.0 0.0 copy-start.2
  18.0 0.8 copy-done.2
  18.8 32.2 %all-to-all-done = f32[128,40,128]{2,1,0:T(8,128)S(1)} async-done(((f32[128,40,128]{2,1,0:T(8,128)}), f32[128,40,128]{2,1,0:T(8,128)S(1)}, u32[]{:S(2)}, u32[]{:S(2)}) %all-to-all-start) | async-done | bytes 2621472 | tf_op jit(solution)/shard_map/all_to_all | solution.py:416
  51.0 1.0 copy-done.3
  52.1 11.8 %deblur.1 = f32[5248,128]{1,0:T(8,128)S(1)} custom-call(f32[5120,128]{1,0:T(8,128)S(1)} %bitcast.17, bf16[256,256]{1,0:T(8,128)(2,1)S(1)} %get-tuple-element.8.sf_ref, bf16[256,256]{1,0:T(8,128)(2,1)S(1)} %get-tuple-element.9.sa_ref, bf16[1024,256]{1,0:T(8,128)(2,1)S(1)} %get-tuple-element.10.wf_ref, bf16[1024,256]{1,0:T(8,128)(2,1)S(1)} %copy-done.3), custom_call_target="tpu_custom_call" | custom-call | flops 5000000000 | bytes 15000000 | tf_op jit(solution)/shard_map/deblur/pallas_call | solution.py:417
  63.8 41.0 %all_to_all.15 = f32[128,41,1,128]{3,2,1,0:T(1,128)S(1)} all-to-all(f32[128,41,1,128]{3,2,1,0:T(1,128)S(1)} %bitcast.16), channel_id=1, replica_groups=mesh['rt'=32,'mob'=4] {'rt','mob'}, dimensions={0} | all-to-all | bytes 5373952 | tf_op jit(solution)/shard_map/all_to_all | solution.py:435
  104.9 0.7 cross.1
  105.5 0.0 copy-start.4
  105.5 0.0 copy-start.5
  105.6 0.2 collective-permute-start
  105.7 1.8 %collective-permute-done = f32[32,2,8,256]{3,2,1,0:T(8,128)S(1)} collective-permute-done((f32[32,2,8,256]{3,2,1,0:T(8,128)S(1)}, f32[32,2,8,256]{3,2,1,0:T(8,128)S(1)}, u32[]{:S(2)}, u32[]{:S(2)}) %collective-permute-start) | collective-permute-done | bytes 524320 | tf_op jit(solution)/shard_map/ppermute | solution.py:442
  107.5 0.9 add.3
  108.4 5.8 %all-to-all-start.2 = ((f32[64,8,256]{2,1,0:T(8,128)}), f32[64,8,256]{2,1,0:T(8,128)S(1)}, u32[]{:S(2)}, u32[]{:S(2)}) async-start(f32[64,8,256]{2,1,0:T(8,128)} %bitcast.18), calls=%async_computation.2 | async-start | bytes 1048576 | tf_op jit(solution)/shard_map/all_to_all | solution.py:444
  114.3 0.1 compare_convert_fusion.mask_ref
  114.3 3.9 %unpack.1 = f32[5120,128]{1,0:T(8,128)} custom-call(f32[5248,128]{1,0:T(8,128)S(1)} %bitcast.15), custom_call_target="tpu_custom_call" | custom-call | flops 5000000000 | bytes 15000000 | tf_op jit(solution)/shard_map/unpack/pallas_call | solution.py:447
  118.2 8.4 %all-to-all-done.2.sums_ref = f32[64,8,256]{2,1,0:T(8,128)S(1)} async-done(((f32[64,8,256]{2,1,0:T(8,128)}), f32[64,8,256]{2,1,0:T(8,128)S(1)}, u32[]{:S(2)}, u32[]{:S(2)}) %all-to-all-start.2) | async-done | bytes 524320 | tf_op jit(solution)/shard_map/all_to_all | solution.py:444
  126.6 0.7 finish.1
  (3 shorter events, 0.0 us)
Async XLA Ops:
  3.9 11.5 %copy-start = (f32[31]{0:T(128)S(1)}, f32[31]{0:T(128)}, u32[]{:S(2)}) copy-start(f32[31]{0:T(128)} %frame_ref.1) | copy-start | bytes 376
  3.9 11.5 %copy-start.1 = (f32[15]{0:T(128)S(1)}, f32[15]{0:T(128)}, u32[]{:S(2)}) copy-start(f32[15]{0:T(128)} %scan_ref.1) | copy-start | bytes 184
  3.9 47.1 %all-to-all-start = ((f32[128,40,128]{2,1,0:T(8,128)}), f32[128,40,128]{2,1,0:T(8,128)S(1)}, u32[]{:S(2)}, u32[]{:S(2)}) async-start(f32[128,40,128]{2,1,0:T(8,128)} %pack.1), calls=%async_computation | async-start | bytes 5242880 | tf_op jit(solution)/shard_map/all_to_all | solution.py:416
  18.0 0.8 copy-start.2
  51.0 1.0 copy-start.3
  105.5 8.7 %copy-start.4 = (s32[256]{0:T(256)S(1)}, s32[256]{0:T(256)}, u32[]{:S(2)}) copy-start(s32[256]{0:T(256)} %param.9) | copy-start | bytes 3076
  105.5 8.7 %copy-start.5 = (s32[8]{0:T(128)S(1)}, s32[8]{0:T(128)}, u32[]{:S(2)}) copy-start(s32[8]{0:T(128)} %param.8) | copy-start | bytes 100
  105.6 2.0 %collective-permute-start = (f32[32,2,8,256]{3,2,1,0:T(8,128)S(1)}, f32[32,2,8,256]{3,2,1,0:T(8,128)S(1)}, u32[]{:S(2)}, u32[]{:S(2)}) collective-permute-start(f32[32,2,8,256]{3,2,1,0:T(8,128)S(1)} %get-tuple-element.13), channel_id=1, source_target_pairs={{0,1},{1,0},{2,3},{3,2},{4,5},{5,4},{6,7},{7,6},{8,9},{9,8},{10,11... | collective-permute-start | bytes 1572872 | tf_op jit(solution)/shard_map/ppermute | solution.py:442
  108.4 18.1 %all-to-all-start.2 = ((f32[64,8,256]{2,1,0:T(8,128)}), f32[64,8,256]{2,1,0:T(8,128)S(1)}, u32[]{:S(2)}, u32[]{:S(2)}) async-start(f32[64,8,256]{2,1,0:T(8,128)} %bitcast.18), calls=%async_computation.2 | async-start | bytes 1048576 | tf_op jit(solution)/shard_map/all_to_all | solution.py:444

commit v7 on v6

--- a/solution.py
+++ b/solution.py
@@ -106,7 +106,7 @@
         _, edge_low = split(
             taps_at(sign * (edge_again - edge_target) + frame_radius, frame_ref, 2 * frame_radius + 1)
         )
-        pieces = (high, high, low, jnp.where(again, edge_low, edge_high), edge_high)
+        pieces = (high, low, jnp.where(again, edge_low, edge_high), edge_high)
         at = 0
         for piece in pieces:
             ref[at : at + piece.shape[0], :] = piece
@@ -201,7 +201,8 @@
             here = slice(first * group, (first + count) * group)
             center, rest = ref[u, here, 0 : 2 * width], ref[u, here, 2 * width : 2 * width + 2 * HALO]
             lhs.append(jnp.concatenate([center, center[:, 0:width], rest], axis=1))
-        out = jnp.dot(jnp.concatenate(lhs, axis=0), matrix, preferred_element_type=F32)
+        rhs = jnp.concatenate([matrix[0:width, :], matrix[...]], axis=0)
+        out = jnp.dot(jnp.concatenate(lhs, axis=0), rhs, preferred_element_type=F32)
         places = [(u, first + n) for u, first, count in chunks for n in range(count)]
         return [(u, n, out[i * group : (i + 1) * group]) for i, (u, n) in enumerate(places)]
 
@@ -244,11 +245,11 @@
         put_halo(left_ref, u)
 
     def ratios(chunks):
-        for u, n, blurred in frame_blur(left_ref, chunks, wf_ref[...]):
+        for u, n, blurred in frame_blur(left_ref, chunks, wf_ref):
             put(back_ref, u, n, obs_ref[u, n] / blurred)
 
     def adjoint_frames(chunks):
-        for u, n, blurred in frame_blur(back_ref, chunks, wa_ref[...]):
+        for u, n, blurred in frame_blur(back_ref, chunks, wa_ref):
             put(left_ref, u, n, blurred)
 
     def adjoint_scans(u, iteration):
@@ -367,7 +368,7 @@
     width = (channels - PREC) // mobs
     vmem = pl.BlockSpec(memory_space=pltpu.VMEM)
     smem = pl.BlockSpec(memory_space=pltpu.SMEM)
-    depth = 3 * BLOCK + 2 * HALO
+    depth = 2 * BLOCK + 2 * HALO
 
     hbm = pl.BlockSpec(memory_space=pltpu.HBM)
 

time: 128 us -> 128 us (level)
  no operation moved by 1% of the time
where the time goes in v7:
time: 128 us; the launch traced here: 127 us
  waiting for transfers between devices  42.6 us (33%)
  blocking collectives  41 us (32%)
  Pallas kernels  22.8 us (18%)
  starting transfers between devices  17.5 us (14%)
  local copies, waits for them, and re-layouts  1.57 us (1%)
    all_to_all x1, blocking collectives, local(): lax.all_to_all(deblurred.reshape(owners, out_rows // STATS, STATS, LANES)...  41 us
    all_to_all x1, waiting for transfers between devices, local(): arrived = lax.all_to_all(packed, AXES, 0, 0, tiled=True)  32.4 us
    pallas_call x1, Pallas kernels, local(): call(deblur_kernel, 'deblur', shape((owners * out_rows, LANES), F32), [vm...  11.8 us
    all_to_all x1, starting transfers between devices, local(): arrived = lax.all_to_all(packed, AXES, 0, 0, tiled=True)  11.5 us
    all_to_all x1, waiting for transfers between devices, local(): lax.all_to_all(both.reshape(owners // CORES, PREC // row_shards, width),...  8.36 us
    all_to_all x1, starting transfers between devices, local(): lax.all_to_all(both.reshape(owners // CORES, PREC // row_shards, width),...  5.81 us
    pallas_call x1, Pallas kernels, local(): call(unpack_kernel, 'unpack', shape((cells * channels // LANES, LANES), F...  3.85 us
    pallas_call x1, Pallas kernels, local(): call(pack_kernel, 'pack', shape((owners, rows, LANES), F32), [hbm], [pltp...  3.27 us
  transfers between devices with their start and end apart: 3, of which 3 were waited for; matrix products, arithmetic and copies ran while one was open for 0% of the time, Pallas kernels for 5%

profile of v7, /device:TPU:1, one launch (start us, length us, event | category | flops | bytes accessed | tf_op | source)
XLA Modules:
  0.0 127.1 jit_solution(177878174651517197)
XLA Ops:
  0.6 3.3 %pack.1 = f32[128,40,128]{2,1,0:T(8,128)} custom-call(f32[64,10,8,128]{3,2,1,0:T(8,128)} %bitcast.19), custom_call_target="tpu_custom_call" | custom-call | flops 5000000000 | bytes 15000000 | tf_op jit(solution)/shard_map/pack/pallas_call | solution.py:392
  3.9 0.0 copy-start
  3.9 0.0 copy-start.1
  3.9 11.5 %all-to-all-start = ((f32[128,40,128]{2,1,0:T(8,128)}), f32[128,40,128]{2,1,0:T(8,128)S(1)}, u32[]{:S(2)}, u32[]{:S(2)}) async-start(f32[128,40,128]{2,1,0:T(8,128)} %pack.1), calls=%async_computation | async-start | bytes 5242880 | tf_op jit(solution)/shard_map/all_to_all | solution.py:417
  15.4 0.0 copy-done
  15.4 0.0 copy-done.1
  15.4 2.6 %bands.1 = (bf16[256,256]{1,0:T(8,128)(2,1)S(1)}, bf16[256,256]{1,0:T(8,128)(2,1)S(1)}, bf16[768,256]{1,0:T(8,128)(2,1)S(1)}, bf16[768,256]{1,0:T(8,128)(2,1)S(1)}) custom-call(f32[31]{0:T(128)S(1)} %copy-done, f32[15]{0:T(128)S(1)} %copy-done.1), custom_call_target="tpu_custom_call" | custom-call | flops 5000000000 | bytes 15000000 | tf_op jit(solution)/shard_map/bands/pallas_call | solution.py:408
  18.0 0.0 copy-start.2
  18.0 0.6 copy-done.2
  18.7 32.4 %all-to-all-done = f32[128,40,128]{2,1,0:T(8,128)S(1)} async-done(((f32[128,40,128]{2,1,0:T(8,128)}), f32[128,40,128]{2,1,0:T(8,128)S(1)}, u32[]{:S(2)}, u32[]{:S(2)}) %all-to-all-start) | async-done | bytes 2621472 | tf_op jit(solution)/shard_map/all_to_all | solution.py:417
  51.0 0.9 copy-done.3
  51.9 11.8 %deblur.1 = f32[5248,128]{1,0:T(8,128)S(1)} custom-call(f32[5120,128]{1,0:T(8,128)S(1)} %bitcast.17, bf16[256,256]{1,0:T(8,128)(2,1)S(1)} %get-tuple-element.8.sf_ref, bf16[256,256]{1,0:T(8,128)(2,1)S(1)} %copy-done.3, bf16[768,256]{1,0:T(8,128)(2,1)S(1)} %get-tuple-element.10.wf_ref, bf16[768,256]{1,0:T(8,128)(2,1)S(1)} %get-tuple-element.11.wa_ref), custom_call_target="tpu_custom_call" | custom-call | flops 5000000000 | bytes 15000000 | tf_op jit(solution)/shard_map/deblur/pallas_call | solution.py:418
  63.7 41.0 %all_to_all.15 = f32[128,41,1,128]{3,2,1,0:T(1,128)S(1)} all-to-all(f32[128,41,1,128]{3,2,1,0:T(1,128)S(1)} %bitcast.16), channel_id=1, replica_groups=mesh['rt'=32,'mob'=4] {'rt','mob'}, dimensions={0} | all-to-all | bytes 5373952 | tf_op jit(solution)/shard_map/all_to_all | solution.py:436
  104.8 0.7 cross.1
  105.4 0.0 copy-start.4
  105.4 0.0 copy-start.5
  105.4 0.2 collective-permute-start
  105.6 1.8 %collective-permute-done = f32[32,2,8,256]{3,2,1,0:T(8,128)S(1)} collective-permute-done((f32[32,2,8,256]{3,2,1,0:T(8,128)S(1)}, f32[32,2,8,256]{3,2,1,0:T(8,128)S(1)}, u32[]{:S(2)}, u32[]{:S(2)}) %collective-permute-start) | collective-permute-done | bytes 524320 | tf_op jit(solution)/shard_map/ppermute | solution.py:443
  107.4 0.9 add.3
  108.3 5.8 %all-to-all-start.2 = ((f32[64,8,256]{2,1,0:T(8,128)}), f32[64,8,256]{2,1,0:T(8,128)S(1)}, u32[]{:S(2)}, u32[]{:S(2)}) async-start(f32[64,8,256]{2,1,0:T(8,128)} %bitcast.18), calls=%async_computation.2 | async-start | bytes 1048576 | tf_op jit(solution)/shard_map/all_to_all | solution.py:445
  114.2 0.1 compare_convert_fusion.mask_ref
  114.2 3.9 %unpack.1 = f32[5120,128]{1,0:T(8,128)} custom-call(f32[5248,128]{1,0:T(8,128)S(1)} %bitcast.15), custom_call_target="tpu_custom_call" | custom-call | flops 5000000000 | bytes 15000000 | tf_op jit(solution)/shard_map/unpack/pallas_call | solution.py:448
  118.1 8.4 %all-to-all-done.2.sums_ref = f32[64,8,256]{2,1,0:T(8,128)S(1)} async-done(((f32[64,8,256]{2,1,0:T(8,128)}), f32[64,8,256]{2,1,0:T(8,128)S(1)}, u32[]{:S(2)}, u32[]{:S(2)}) %all-to-all-start.2) | async-done | bytes 524320 | tf_op jit(solution)/shard_map/all_to_all | solution.py:445
  126.4 0.7 finish.1
  (3 shorter events, 0.0 us)
Async XLA Ops:
  3.9 11.5 %copy-start = (f32[31]{0:T(128)S(1)}, f32[31]{0:T(128)}, u32[]{:S(2)}) copy-start(f32[31]{0:T(128)} %frame_ref.1) | copy-start | bytes 376
  3.9 11.5 %copy-start.1 = (f32[15]{0:T(128)S(1)}, f32[15]{0:T(128)}, u32[]{:S(2)}) copy-start(f32[15]{0:T(128)} %scan_ref.1) | copy-start | bytes 184
  3.9 47.1 %all-to-all-start = ((f32[128,40,128]{2,1,0:T(8,128)}), f32[128,40,128]{2,1,0:T(8,128)S(1)}, u32[]{:S(2)}, u32[]{:S(2)}) async-start(f32[128,40,128]{2,1,0:T(8,128)} %pack.1), calls=%async_computation | async-start | bytes 5242880 | tf_op jit(solution)/shard_map/all_to_all | solution.py:417
  18.0 0.7 copy-start.2
  51.0 0.9 copy-start.3
  105.4 8.7 %copy-start.4 = (s32[256]{0:T(256)S(1)}, s32[256]{0:T(256)}, u32[]{:S(2)}) copy-start(s32[256]{0:T(256)} %param.9) | copy-start | bytes 3076
  105.4 8.7 %copy-start.5 = (s32[8]{0:T(128)S(1)}, s32[8]{0:T(128)}, u32[]{:S(2)}) copy-start(s32[8]{0:T(128)} %param.8) | copy-start | bytes 100
  105.4 2.0 %collective-permute-start = (f32[32,2,8,256]{3,2,1,0:T(8,128)S(1)}, f32[32,2,8,256]{3,2,1,0:T(8,128)S(1)}, u32[]{:S(2)}, u32[]{:S(2)}) collective-permute-start(f32[32,2,8,256]{3,2,1,0:T(8,128)S(1)} %get-tuple-element.13), channel_id=1, source_target_pairs={{0,1},{1,0},{2,3},{3,2},{4,5},{5,4},{6,7},{7,6},{8,9},{9,8},{10,11... | collective-permute-start | bytes 1572872 | tf_op jit(solution)/shard_map/ppermute | solution.py:443
  108.3 18.1 %all-to-all-start.2 = ((f32[64,8,256]{2,1,0:T(8,128)}), f32[64,8,256]{2,1,0:T(8,128)S(1)}, u32[]{:S(2)}, u32[]{:S(2)}) async-start(f32[64,8,256]{2,1,0:T(8,128)} %bitcast.18), calls=%async_computation.2 | async-start | bytes 1048576 | tf_op jit(solution)/shard_map/all_to_all | solution.py:445
